TPU v7x, 256 devices: a whole 4x4x8 slice. The times are simulated.
256 devices in a mesh: tile: 64 (over y, z, core), depth: 4 (over x).
Axes of the slice: x: 4, y: 4, z: 8, core: 2. Of those that a mesh axis runs over, the one named last changes fastest.
Arguments:
- features: bfloat16 [8192, 128, 128], P('tile'), may hold values from -6 to 6
- geometry: float32 [8192, 6, 128], P('tile'), may hold values from -3 to 4114, as said below
- send_lists: int32 [64, 64, 2], P('tile'), may hold values from 0 to 127, as said below
- tile_ids: int32 [256], P('tile'), may hold values from 0 to 255, as said below
- tile_lists: int32 [256, 8, 8], P('tile', 'depth'), may hold values from 0 to 127, as said below
- live_counts: int32 [256, 8], P('tile', 'depth'), may hold values from 5 to 8, as said below
- cotangent: bfloat16 [256, 256, 128], P('tile'), may hold values from -6 to 6
Outputs:
- image_out: bfloat16 [256, 256, 128], P('tile', 'depth')
- feature_grads: float32 [8192, 128, 128], P('tile', 'depth')
- geometry_grads: float32 [8192, 6, 128], P('tile', None, 'depth')
Inputs may be any that keep to these rules, and one draw needn't show every extreme that they name: send_lists[s, t, j] is the local block of owner s in slot j of its bucket for tile index t; the 2 entries of one (s, t) are distinct, and each owner hands out its blocks in a fixed order of its own, repeated, so its blocks are sent equally often up to one. A permutation: tile slot u covers image columns 16 tile_ids[u] to 16 tile_ids[u] + 15 of a band 16 pixels high. tile_lists[u, g, k] = s * 2 + j names block j of the bucket that owner s sends to the tile index holding u; each tile index's 4 * 8 * 8 entries run through an order of its own of its 128 slots, repeated, so every slot is named equally often up to one. Entries at k >= live_counts[u, g] are ignored. `geometry`: Rows: mean x and y in pixels, inverse covariance a, b, c with a > 0, c > 0, a c > b^2, and opacity in (0, 0.9].
All inputs are finite; a program needn't handle non-finite values.
Results may differ from a plain program's by a relative error of at most 0.0085.
Values may be sent and summed in bfloat16 or wider, within the bound.
A program may use at most 64 MiB of HBM per device.

v0:
```python
import jax
import jax.numpy as jnp
from jax import lax
from jax.sharding import PartitionSpec as P

precise = lax.Precision.HIGHEST


def entering(value, axis, combine, identity, reverse):
    size, index = (lax.axis_size(axis), lax.axis_index(axis))
    everything = jax.tree.map(lambda part: lax.all_gather(part, axis), value)
    start = jax.tree.map(
        lambda part, zero: jnp.broadcast_to(jnp.asarray(zero, part.dtype), part.shape),
        value,
        identity,
    )

    def turn(k, before):
        at = size - 1 - k if reverse else k
        reached = at > index if reverse else at < index
        new = combine(before, jax.tree.map(lambda part: part[at], everything))
        return jax.tree.map(lambda a, b: jnp.where(reached, a, b), new, before)

    return lax.fori_loop(0, size, turn, start)


def cut_along(value, dim, size):
    before, after = (value.shape[:dim], value.shape[dim + 1 :])
    return jnp.moveaxis(value.reshape(*before, size, -1, *after), dim, 0)


def summed_on_arrival(value, axis, dim):
    parts = cut_along(value, dim, lax.axis_size(axis))
    arrived = lax.all_to_all(parts, axis, split_axis=0, concat_axis=0, tiled=True)
    return arrived.sum(axis=0)


def strict_before(count):
    row_ids = lax.broadcasted_iota(jnp.int32, (count, count), 0)
    col_ids = lax.broadcasted_iota(jnp.int32, (count, count), 1)
    return (row_ids < col_ids).astype(jnp.float32)


def along_gauss(values, matrix):
    flat = values.reshape(-1, values.shape[-1])
    return jnp.dot(flat, matrix, precision=precise, preferred_element_type=jnp.float32).reshape(
        values.shape
    )


def shape_terms(block_shape, px_rows, py_rows, live_mask):
    delta_x = px_rows[:, :, None] - block_shape[:, 0, None, :]
    delta_y = py_rows[:, :, None] - block_shape[:, 1, None, :]
    conic_a = block_shape[:, 2, None, :]
    conic_b = block_shape[:, 3, None, :]
    conic_c = block_shape[:, 4, None, :]
    quadric = (
        conic_a * delta_x * delta_x
        + 2.0 * conic_b * delta_x * delta_y
        + conic_c * delta_y * delta_y
    )
    falloff = jnp.exp(-0.5 * quadric)
    alphas = block_shape[:, 5, None, :] * falloff * live_mask[:, None, None]
    return (delta_x, delta_y, conic_a, conic_b, conic_c, falloff, alphas)


def pick_rows(selector, values):
    return lax.dot_general(
        selector,
        values,
        (((0,), (0,)), ((), ())),
        precision=precise,
        preferred_element_type=jnp.float32,
    )


def multiply_light(earlier, later):
    return earlier * later


def behind_pair(earlier, later):
    return (later[0] * earlier[0], later[1] + later[0] * earlier[1])


def local(features, geometry, send_lists, tile_ids, tile_lists, live_counts, cotangent):
    tile_count = lax.axis_size("tile")
    depth_count = lax.axis_size("depth")
    depth_index = lax.axis_index("depth")
    block_count, gauss_count, feat_count = features.shape
    capacity = send_lists.shape[2]
    pool_size = tile_count * capacity
    tiles_here, segs_here, list_len = tile_lists.shape
    pixel_count = cotangent.shape[1]
    batch_rows = tiles_here * segs_here
    quarter = gauss_count // depth_count
    picked = send_lists[0].reshape(pool_size)
    sent_shape = jnp.take(geometry, picked, axis=0).reshape(tile_count, capacity, 6, gauss_count)
    pool_shape = lax.all_to_all(sent_shape, "tile", split_axis=0, concat_axis=0, tiled=True)
    own_feat = lax.dynamic_slice_in_dim(features, depth_index * quarter, quarter, 1)
    sent_feat = jnp.take(own_feat, picked, axis=0).reshape(
        tile_count, capacity, quarter, feat_count
    )
    part_feat = lax.all_to_all(sent_feat, "tile", split_axis=0, concat_axis=0, tiled=True)
    pool_feat = lax.all_gather(part_feat, "depth", axis=2, tiled=True)
    pool_feat = pool_feat.reshape(pool_size, gauss_count, feat_count)
    pool_shape = pool_shape.reshape(pool_size, 6, gauss_count)
    pixel_iota = jnp.arange(pixel_count, dtype=jnp.int32)
    column = (pixel_iota % 16).astype(jnp.float32) + 0.5
    row_pos = (pixel_iota // 16).astype(jnp.float32) + 0.5
    px_tiles = 16.0 * tile_ids.astype(jnp.float32)[:, None] + column[None, :]
    px_rows = jnp.repeat(px_tiles, segs_here, axis=0)
    py_rows = jnp.broadcast_to(row_pos[None, :], (batch_rows, pixel_count))
    slot_table = tile_lists.reshape(batch_rows, list_len).T
    entry_iota = jnp.arange(list_len, dtype=jnp.int32)
    live_table = (entry_iota[:, None] < live_counts.reshape(batch_rows)[None, :]).astype(
        jnp.float32
    )
    before_mat = strict_before(gauss_count)
    after_mat = before_mat.T

    def forward_step(state_pair, inputs):
        log_light, colors = state_pair
        slot_ids, live_mask = inputs
        block_shape = jnp.take(pool_shape, slot_ids, axis=0)
        block_feat = jnp.take(pool_feat, slot_ids, axis=0)
        alphas = shape_terms(block_shape, px_rows, py_rows, live_mask)[6]
        log_keep = jnp.log1p(-alphas)
        inside = jnp.exp(log_light[:, :, None] + along_gauss(log_keep, before_mat))
        weights = (inside * alphas).astype(jnp.bfloat16)
        colors = colors + jnp.einsum(
            "bpg,bgf->bpf", weights, block_feat, preferred_element_type=jnp.float32
        )
        return ((log_light + jnp.sum(log_keep, axis=2), colors), log_light)

    start_pair = (
        jnp.zeros((batch_rows, pixel_count), jnp.float32),
        jnp.zeros((batch_rows, pixel_count, feat_count), jnp.float32),
    )
    (log_light, colors), log_starts = lax.scan(forward_step, start_pair, (slot_table, live_table))
    seg_light = jnp.exp(log_light).reshape(tiles_here, segs_here, pixel_count)
    seg_color = colors.reshape(tiles_here, segs_here, pixel_count, feat_count)
    grads_in = cotangent.astype(jnp.float32)
    seg_dots = jnp.sum(seg_color * grads_in[:, None], axis=3)
    local_light = jnp.ones((tiles_here, pixel_count), jnp.float32)
    local_color = jnp.zeros((tiles_here, pixel_count, feat_count), jnp.float32)
    inner_front = []
    for segment in range(segs_here):
        inner_front.append(local_light)
        local_color = local_color + local_light[:, :, None] * seg_color[:, segment]
        local_light = local_light * seg_light[:, segment]
    local_dot = jnp.sum(local_color * grads_in, axis=2)
    front_light = entering(local_light, "depth", multiply_light, jnp.ones_like(local_light), False)
    image_part = summed_on_arrival(front_light[:, :, None] * local_color, "depth", 1)
    behind = entering(
        (local_light, local_dot),
        "depth",
        behind_pair,
        (jnp.ones_like(local_light), jnp.zeros_like(local_dot)),
        True,
    )
    behind_sum = behind[1]
    image_out = image_part.astype(jnp.bfloat16)
    color_grads = [None] * segs_here
    end_light = [None] * segs_here
    later_sum = behind_sum
    for segment in range(segs_here - 1, -1, -1):
        seg_front = front_light * inner_front[segment]
        color_grads[segment] = (seg_front[:, :, None] * grads_in).astype(jnp.bfloat16)
        end_light[segment] = seg_front * later_sum * seg_light[:, segment]
        later_sum = seg_dots[:, segment] + seg_light[:, segment] * later_sum
    color_grad = jnp.stack(color_grads, axis=1).reshape(batch_rows, pixel_count, feat_count)
    end_value = jnp.stack(end_light, axis=1).reshape(batch_rows, pixel_count)

    def backward_step(suffix, inputs):
        slot_ids, live_mask, log_start = inputs
        block_shape = jnp.take(pool_shape, slot_ids, axis=0)
        block_feat = jnp.take(pool_feat, slot_ids, axis=0)
        delta_x, delta_y, conic_a, conic_b, conic_c, falloff, alphas = shape_terms(
            block_shape, px_rows, py_rows, live_mask
        )
        log_keep = jnp.log1p(-alphas)
        inside = jnp.exp(log_start[:, :, None] + along_gauss(log_keep, before_mat))
        exact_w = inside * alphas
        weights = exact_w.astype(jnp.bfloat16)
        weight_grad = jnp.einsum(
            "bpf,bgf->bpg", color_grad, block_feat, preferred_element_type=jnp.float32
        )
        carried = weight_grad * exact_w
        after_sum = suffix[:, :, None] + along_gauss(carried, after_mat)
        alpha_grad = weight_grad * inside - after_sum / (1.0 - alphas)
        quad_grad = -0.5 * alpha_grad * alphas
        shape_grad = jnp.stack(
            [
                jnp.sum(-2.0 * quad_grad * (conic_a * delta_x + conic_b * delta_y), axis=1),
                jnp.sum(-2.0 * quad_grad * (conic_b * delta_x + conic_c * delta_y), axis=1),
                jnp.sum(quad_grad * delta_x * delta_x, axis=1),
                jnp.sum(2.0 * quad_grad * delta_x * delta_y, axis=1),
                jnp.sum(quad_grad * delta_y * delta_y, axis=1),
                jnp.sum(alpha_grad * falloff * live_mask[:, None, None], axis=1),
            ],
            axis=1,
        )
        feat_grad = jnp.einsum(
            "bpg,bpf->bgf", weights, color_grad, preferred_element_type=jnp.float32
        )
        return (suffix + jnp.sum(carried, axis=2), (feat_grad, shape_grad))

    _, (feat_grads, shape_grads) = lax.scan(
        backward_step, end_value, (slot_table, live_table, log_starts), reverse=True
    )
    flat_slots = slot_table.reshape(list_len * batch_rows)
    pool_iota = jnp.arange(pool_size, dtype=jnp.int32)
    slot_select = (flat_slots[:, None] == pool_iota[None, :]).astype(jnp.float32)
    pool_dfeat = pick_rows(
        slot_select, feat_grads.reshape(list_len * batch_rows, gauss_count * feat_count)
    )
    pool_dshape = pick_rows(
        slot_select, shape_grads.reshape(list_len * batch_rows, 6 * gauss_count)
    )
    owner_select = (picked[:, None] == jnp.arange(block_count, dtype=jnp.int32)[None, :]).astype(
        jnp.float32
    )
    part_dfeat, part_dshape = (
        lax.psum_scatter(
            pool_dfeat.reshape(pool_size, gauss_count, feat_count).astype(jnp.bfloat16),
            "depth",
            scatter_dimension=1,
            tiled=True,
        ).astype(jnp.float32),
        lax.psum_scatter(
            pool_dshape.reshape(pool_size, 6, gauss_count).astype(jnp.bfloat16),
            "depth",
            scatter_dimension=2,
            tiled=True,
        ).astype(jnp.float32),
    )
    back_feat, back_shape = (
        lax.all_to_all(
            part_dfeat.reshape(tile_count, capacity, quarter, feat_count).astype(jnp.bfloat16),
            "tile",
            split_axis=0,
            concat_axis=0,
            tiled=True,
        ).astype(jnp.float32),
        lax.all_to_all(
            part_dshape.reshape(tile_count, capacity, 6, quarter).astype(jnp.bfloat16),
            "tile",
            split_axis=0,
            concat_axis=0,
            tiled=True,
        ).astype(jnp.float32),
    )
    feature_grads = pick_rows(
        owner_select, back_feat.reshape(pool_size, quarter * feat_count)
    ).reshape(block_count, quarter, feat_count)
    geometry_grads = pick_rows(owner_select, back_shape.reshape(pool_size, 6 * quarter)).reshape(
        block_count, 6, quarter
    )
    return (image_out, feature_grads, geometry_grads)


def solution(mesh):
    placed = (
        P("tile", None, None),
        P("tile", None, None),
        P("tile", None, None),
        P("tile"),
        P("tile", "depth", None),
        P("tile", "depth"),
        P("tile", None, None),
    )
    return jax.shard_map(
        local,
        mesh=mesh,
        in_specs=placed,
        out_specs=(P("tile", "depth", None), P("tile", "depth", None), P("tile", None, "depth")),
        check_vma=False,
    )
```

profile of v0, /device:TPU:1, one launch (start us, length us, event | category | flops | bytes accessed | tf_op | source)
XLA Modules:
  0.0 453.8 jit_solution(5572934024064053974)
XLA Ops:
  11.3 41.6 %all_to_all.25 = bf16[64,2,32,128]{3,2,1,0:T(8,128)(2,1)} all-to-all(bf16[64,2,32,128]{3,2,1,0:T(8,128)(2,1)S(1)} %broadcast_select_fusion.3), channel_id=1, replica_groups=mesh['tile'=64,'depth'=4] {'tile'}, dimensions={0} | all-to-all | bytes 2097152 | tf_op jit(solution)/shard_map/all_to_all | solution.py:103
  55.1 6.2 %all-to-all-start = ((f32[64,2,6,128]{3,1,2,0:T(2,128)}), f32[64,2,6,128]{3,1,2,0:T(2,128)S(1)}, u32[]{:S(2)}, u32[]{:S(2)}) async-start(f32[64,2,6,128]{3,1,2,0:T(2,128)} %copy_select_fusion), calls=%async_computation | async-start | bytes 786432 | tf_op jit(solution)/shard_map/all_to_all | solution.py:98
  62.0 13.9 %all-to-all-done = f32[64,2,6,128]{3,1,2,0:T(2,128)S(1)} async-done(((f32[64,2,6,128]{3,1,2,0:T(2,128)}), f32[64,2,6,128]{3,1,2,0:T(2,128)S(1)}, u32[]{:S(2)}, u32[]{:S(2)}) %all-to-all-start) | async-done | bytes 393248 | tf_op jit(solution)/shard_map/all_to_all | solution.py:98
  77.1 23.4 %all-gather.5.cloned.1.call-done = bf16[64,2,128,128]{3,2,1,0:T(8,128)(2,1)} async-done(((bf16[64,2,32,128]{3,2,1,0:T(8,128)(2,1)}), bf16[64,2,128,128]{3,2,1,0:T(8,128)(2,1)}) %all-gather.5.cloned.1.call-update) | async-done | bytes 4194320 | tf_op jit(solution)/shard_map/all_gather | solution.py:104
  100.5 68.5 %while.65 = (s32[]{:T(128)}, f32[8,256]{1,0:T(8,128)S(1)}, f32[8,256,128]{2,1,0:T(8,128)S(1)}, f32[8,8,256]{2,1,0:T(8,128)S(1)}, s32[8,8]{1,0:T(8,128)S(1)}, /*i...) while((s32[]{:T(128)}, f32[8,256]{1,0:T(8,128)S(1)}, ...), condition=%wide.region_2.5_spmd.clone, body=%wide.region_0.4_spmd.clone.sunk | while | flops 482256960 | bytes 4245964 | solution.py:139
  103.3 2.8 gather_fusion.3
  111.9 2.8 gather_fusion.3
  120.5 2.8 gather_fusion.3
  129.0 2.8 gather_fusion.3
  137.6 2.8 gather_fusion.3
  146.1 2.8 gather_fusion.3
  154.7 2.8 gather_fusion.3
  163.3 2.8 gather_fusion.3
  169.4 9.1 %all-gather = f32[16,1,256]{2,1,0:T(1,128)S(1)} all-gather(f32[4,1,256]{2,1,0:T(1,128)S(1)} %copy.136), channel_id=2, replica_groups=mesh['tile'=64,'depth'=4] {'depth'}, dimensions={0}, use_global_device_ids=true | all-gather | bytes 20480 | tf_op jit(solution)/shard_map/all_gather | solution.py:11
  179.3 9.3 %all-gather.2 = f32[4,4,256]{2,1,0:T(4,128)S(1)} all-gather(f32[1,4,256]{2,1,0:T(4,128)S(1)} %bitcast.327), channel_id=3, replica_groups=mesh['tile'=64,'depth'=4] {'depth'}, dimensions={0}, use_global_device_ids=true | all-gather | bytes 20480 | tf_op jit(solution)/shard_map/all_gather | solution.py:11
  191.6 126.1 %while.64 = (s32[]{:T(128)}, f32[8,256]{1,0:T(8,128)S(1)}, f32[8,8,128,128]{3,2,1,0:T(8,128)}, f32[8,8,6,128]{3,2,1,0:T(8,128)S(1)}, s32[8,8]{1,0:T(8,128)S(1)},...) while((s32[]{:T(128)}, f32[8,256]{1,0:T(8,128)S(1)}, ...), condition=%wide.region_18.21_spmd.clone, body=%wide.region_10.20_spmd.clone.sunk | while | flops 966723648 | bytes 14422557 | solution.py:208
  193.4 2.8 gather_fusion.1
  198.8 3.9 multiply_multiply_fusion.4
  202.7 2.6 multiply_reduce_fusion.3
  209.2 2.8 gather_fusion.1
  214.5 3.9 multiply_multiply_fusion.4
  218.5 2.6 multiply_reduce_fusion.3
  224.9 2.8 gather_fusion.1
  230.3 3.9 multiply_multiply_fusion.4
  234.2 2.6 multiply_reduce_fusion.3
  240.7 2.8 gather_fusion.1
  246.1 3.9 multiply_multiply_fusion.4
  250.0 2.6 multiply_reduce_fusion.3
  256.5 2.8 gather_fusion.1
  261.8 3.9 multiply_multiply_fusion.4
  265.8 2.6 multiply_reduce_fusion.3
  272.2 2.8 gather_fusion.1
  277.6 3.9 multiply_multiply_fusion.4
  281.5 2.6 multiply_reduce_fusion.3
  288.0 2.8 gather_fusion.1
  293.4 3.9 multiply_multiply_fusion.4
  297.3 2.6 multiply_reduce_fusion.3
  303.8 2.8 gather_fusion.1
  309.1 3.9 multiply_multiply_fusion.4
  313.1 2.6 multiply_reduce_fusion.3
  319.0 10.5 %fusion.77 = bf16[128,128,128]{2,0,1:T(8,128)(2,1)} fusion(s32[64]{0:T(128)S(1)} %eq.33, f32[8,8,128,128]{3,2,1,0:T(8,128)} %get-tuple-element.555), kind=kOutput, calls=%fused_computation.127 | convolution fusion | flops 1612718080 | bytes 8388864 | tf_op jit(solution)/shard_map/dot_general | solution.py:68
  331.0 3.7 all-to-all-start.2
  334.7 11.2 %reduce-scatter.5.cloned.1.call-done = bf16[128,6,32]{0,2,1:T(8,128)(2,1)} async-done(((bf16[128,6,128]{0,2,1:T(8,128)(2,1)}), bf16[128,6,32]{0,2,1:T(8,128)(2,1)}) %reduce-scatter.5.cloned.1.call-update) | async-done | bytes 49168 | tf_op jit(solution)/shard_map/reduce_scatter | solution.py:230
  347.8 13.0 %all-to-all-start.4 = ((bf16[64,2,192]{2,1,0:T(2,128)(2,1)}), bf16[64,2,192]{2,1,0:T(2,128)(2,1)S(1)}, u32[]{:S(2)}, u32[]{:S(2)}) async-start(bf16[64,2,192]{2,1,0:T(2,128)(2,1)} %reshape.326), calls=%async_computation.6 | async-start | bytes 131072 | tf_op jit(solution)/shard_map/all_to_all | solution.py:245
  360.8 39.6 %reduce-scatter.3.cloned.1.call-done = bf16[128,32,128]{2,0,1:T(8,128)(2,1)} async-done(((bf16[128,128,128]{2,0,1:T(8,128)(2,1)}), bf16[128,32,128]{2,0,1:T(8,128)(2,1)}) %reduce-scatter.3.cloned.1.call-update) | async-done | bytes 1048592 | tf_op jit(solution)/shard_map/reduce_scatter | solution.py:224
  400.4 3.4 copy.147
  403.8 10.7 %all-to-all-start.3 = ((bf16[64,2,32,128]{3,2,1,0:T(8,128)(2,1)}), bf16[64,2,32,128]{3,2,1,0:T(8,128)(2,1)S(1)}, u32[]{:S(2)}, u32[]{:S(2)}) async-start(bf16[64,2,32,128]{3,2,1,0:T(8,128)(2,1)} %copy.147), calls=%async_computation.4 | async-start | bytes 2097152 | tf_op jit(solution)/shard_map/all_to_all | solution.py:238
  416.7 26.4 %all-to-all-done.3 = bf16[64,2,32,128]{3,2,1,0:T(8,128)(2,1)S(1)} async-done(((bf16[64,2,32,128]{3,2,1,0:T(8,128)(2,1)}), bf16[64,2,32,128]{3,2,1,0:T(8,128)(2,1)S(1)}, u32[]{:S(2)}, u32[]{:S(2)}) %all-to-all-start.3) | async-done | bytes 1048608 | tf_op jit(solution)/shard_map/all_to_all | solution.py:238
  (320 shorter events, 119.1 us)
Async XLA Ops:
  7.2 45.8 %copy-start = (f32[128,6,128]{2,0,1:T(8,128)S(1)}, f32[128,6,128]{2,0,1:T(8,128)}, u32[]{:S(2)}) copy-start(f32[128,6,128]{2,0,1:T(8,128)} %param.20) | copy-start | bytes 1179652
  7.2 93.3 %all-gather.5.cloned.1.call-start = ((), (), s32[]{:S(2)}) async-start(), calls=%async_computation.7 | async-start | bytes 5242880 | tf_op jit(solution)/shard_map/all_gather | solution.py:104
  52.9 8.6 %copy-start.3 = (s32[4,2]{0,1:T(2,128)S(1)}, s32[4,2]{0,1:T(2,128)}, u32[]{:S(2)}) copy-start(s32[4,2]{0,1:T(2,128)} %param.24) | copy-start | bytes 100
  52.9 8.7 %copy-start.2 = (s32[4,2,8]{2,1,0:T(2,128)S(1)}, s32[4,2,8]{2,1,0:T(2,128)}, u32[]{:S(2)}) copy-start(s32[4,2,8]{2,1,0:T(2,128)} %param.23) | copy-start | bytes 772
  52.9 8.9 %copy-start.1 = (bf16[4,256,128]{2,1,0:T(8,128)(2,1)S(1)}, bf16[4,256,128]{2,1,0:T(8,128)(2,1)}, u32[]{:S(2)}) copy-start(bf16[4,256,128]{2,1,0:T(8,128)(2,1)} %param.25) | copy-start | bytes 786436
  52.9 9.0 %copy-start.4 = (s32[4]{0:T(128)S(1)}, s32[4]{0:T(128)}, u32[]{:S(2)}) copy-start(s32[4]{0:T(128)} %param.22) | copy-start | bytes 52
  55.1 20.8 %all-to-all-start = ((f32[64,2,6,128]{3,1,2,0:T(2,128)}), f32[64,2,6,128]{3,1,2,0:T(2,128)S(1)}, u32[]{:S(2)}, u32[]{:S(2)}) async-start(f32[64,2,6,128]{3,1,2,0:T(2,128)} %copy_select_fusion), calls=%async_computation | async-start | bytes 786432 | tf_op jit(solution)/shard_map/all_to_all | solution.py:98
  61.3 284.6 %reduce-scatter.5.cloned.1.call-start = ((), (), s32[]{:S(2)}) async-start(), calls=%async_computation.9 | async-start | bytes 245760 | tf_op jit(solution)/shard_map/reduce_scatter | solution.py:230
  319.0 81.4 %reduce-scatter.3.cloned.1.call-start = ((), (), s32[]{:S(2)}) async-start(), calls=%async_computation.8 | async-start | bytes 5242880 | tf_op jit(solution)/shard_map/reduce_scatter | solution.py:224
  331.0 16.9 %all-to-all-start.2 = ((f32[4,4,64,128]{3,2,1,0:T(8,128)}), f32[4,4,64,128]{3,2,1,0:T(8,128)S(1)}, u32[]{:S(2)}, u32[]{:S(2)}) async-start(f32[4,4,64,128]{3,2,1,0:T(8,128)} %copy.138), calls=%async_computation.2 | async-start | bytes 1048576 | tf_op jit(solution)/shard_map/all_to_all | solution.py:34
  347.8 56.0 %all-to-all-start.4 = ((bf16[64,2,192]{2,1,0:T(2,128)(2,1)}), bf16[64,2,192]{2,1,0:T(2,128)(2,1)S(1)}, u32[]{:S(2)}, u32[]{:S(2)}) async-start(bf16[64,2,192]{2,1,0:T(2,128)(2,1)} %reshape.326), calls=%async_computation.6 | async-start | bytes 131072 | tf_op jit(solution)/shard_map/all_to_all | solution.py:245
  403.8 39.3 %all-to-all-start.3 = ((bf16[64,2,32,128]{3,2,1,0:T(8,128)(2,1)}), bf16[64,2,32,128]{3,2,1,0:T(8,128)(2,1)S(1)}, u32[]{:S(2)}, u32[]{:S(2)}) async-start(bf16[64,2,32,128]{3,2,1,0:T(8,128)(2,1)} %copy.147), calls=%async_computation.4 | async-start | bytes 2097152 | tf_op jit(solution)/shard_map/all_to_all | solution.py:238
Sparse Core Ops, SparseCore 0:
  53.0 47.3 all-gather.4
  319.1 26.7 reduce-scatter.4
  348.5 51.8 reduce-scatter.2
where the time goes:
time: 456 us; the launch traced here: 454 us
  waiting for transfers between devices  115 us (25%)
  matrix products  104 us (23%)
  local copies, waits for them, and re-layouts  90.1 us (20%)
  blocking collectives  60 us (13%)
  other arithmetic  35.8 us (8%)
  starting transfers between devices  33.7 us (7%)
  between operations  14.1 us (3%)
    dot_general x24, matrix products, along_gauss(): jnp.dot(flat, matrix, precision=precise, preferred_element_type=jnp.float32)  66.7 us
    all_to_all x1, blocking collectives, local(): lax.all_to_all(sent_feat, 'tile', split_axis=0, concat_axis=0, tiled=True)  41.6 us
    reduce_scatter x1, waiting for transfers between devices, local(): lax.psum_scatter(pool_dfeat.reshape(pool_size, gauss_count, feat_count).a...  39.6 us
    all_to_all x1, waiting for transfers between devices, local(): lax.all_to_all(part_dfeat.reshape(tile_count, capacity, quarter, feat_cou...  26.4 us
    all_gather x1, waiting for transfers between devices, local(): pool_feat = lax.all_gather(part_feat, 'depth', axis=2, tiled=True)  23.4 us
    gather x8, local copies, waits for them, and re-layouts, forward_step(): block_feat = jnp.take(pool_feat, slot_ids, axis=0)  22.3 us
    gather x8, local copies, waits for them, and re-layouts, backward_step(): block_feat = jnp.take(pool_feat, slot_ids, axis=0)  22.3 us
    reduce_sum x8, other arithmetic, backward_step(): jnp.sum(alpha_grad * falloff * live_mask[:, None, None], axis=1)  20.9 us
  transfers between devices with their start and end apart: 7, of which 5 were waited for; matrix products, arithmetic and copies ran while one was open for 5% of the time, Pallas kernels for 0%

commit v1 on v0

v1 whole, which is shorter than its diff:
```python
import functools

import jax
import jax.numpy as jnp
from jax import lax
from jax.experimental import pallas as pl
from jax.experimental.pallas import tpu as pltpu
from jax.sharding import PartitionSpec as P

MESH = pl.DeviceIdType.MESH
F32 = jnp.float32
BF16 = jnp.bfloat16
I32 = jnp.int32


def iota(shape, dim):
    return lax.broadcasted_iota(I32, shape, dim)


def ones_where(mask):
    return jnp.where(mask, 1.0, 0.0).astype(BF16)


def split_two(value):
    high = value.astype(BF16)
    low = (value - high.astype(F32)).astype(BF16)
    return high, low


def splat_kernel(
    nt,
    nd,
    cap,
    features,
    geo_own,
    lists_own,
    picked,
    tile_ids,
    cot,
    image_out,
    grad_rx,
    ggeo_rx,
    own_feat,
    feat_tx,
    feat_rx,
    feat_list,
    geo_tx,
    geo_rx,
    lists_rx,
    inv_vec,
    lists_sm,
    inv_sm,
    geo_part,
    geo,
    fall,
    chain,
    later,
    weights,
    light_rx,
    carry_rx,
    offs,
    grad_list,
    grad_tx,
    ggeo,
    ggeo_list,
    ggeo_tx,
    image_part,
    image_rx,
    local_sem,
    geo_sem,
    feat_sem,
    grad_sem,
    ggeo_sem,
    lists_send,
    lists_recv,
    light_send,
    light_recv,
    carry_send,
    carry_recv,
    image_send,
    image_recv,
):
    me = lax.axis_index("tile")
    my = lax.axis_index("depth")
    slots = nt * cap

    barrier = pltpu.get_barrier_semaphore()

    def greet(i, c):
        pl.semaphore_signal(
            barrier, inc=1, device_id={"tile": lax.rem(me + i, nt)}, device_id_type=MESH
        )
        return c

    lax.fori_loop(1, nt, greet, 0)
    for step in range(1, nd):
        pl.semaphore_signal(
            barrier, inc=1, device_id={"depth": lax.rem(my + step, nd)}, device_id_type=MESH
        )

    fetch = pltpu.make_async_copy(
        features.at[:, pl.ds(pl.multiple_of(my * 32, 32), 32), :], own_feat, local_sem.at[0]
    )
    fetch.start()

    def pick_geo(k, c):
        geo_tx[k] = geo_own[picked[k]]
        return c

    lax.fori_loop(0, slots, pick_geo, 0, unroll=8)
    mine = pl.multiple_of(me * cap, cap)
    geo_rx[pl.ds(mine, cap)] = geo_tx[pl.ds(mine, cap)]
    lists_rx[my] = lists_own[...]
    fetch.wait()

    def pick_feat(k, c):
        feat_tx[k] = own_feat[picked[k]]
        return c

    lax.fori_loop(0, slots, pick_feat, 0, unroll=8)
    feat_rx[pl.ds(mine, cap)] = feat_tx[pl.ds(mine, cap)]
    for par in range(2):
        light_rx[par, my] = jnp.zeros((256, 128), F32)
        carry_rx[par, my] = jnp.zeros((256, 128), F32)
    image_part[...] = jnp.zeros(image_part.shape, F32)

    pl.semaphore_wait(barrier, nt - 1 + nd - 1)

    def across_depth(source, target, send, recv, step):
        peer = lax.rem(my + step, nd)
        return pltpu.make_async_remote_copy(
            src_ref=source(peer),
            dst_ref=target,
            send_sem=send.at[peer],
            recv_sem=recv.at[my],
            device_id={"depth": peer},
            device_id_type=MESH,
        )

    def arrived_depth(buffer, send, recv, step):
        other = lax.rem(my + step, nd)
        return pltpu.make_async_remote_copy(
            src_ref=buffer(other),
            dst_ref=buffer(other),
            send_sem=send.at[other],
            recv_sem=recv.at[other],
            device_id={"depth": other},
            device_id_type=MESH,
        )

    def scatter_tiles(source, target, sem):
        def send(i, c):
            peer = lax.rem(me + i, nt)
            there = pl.multiple_of(peer * cap, cap)
            pltpu.make_async_remote_copy(
                src_ref=source.at[pl.ds(there, cap)],
                dst_ref=target.at[pl.ds(mine, cap)],
                send_sem=sem.at[0],
                recv_sem=sem.at[1],
                device_id={"tile": peer},
                device_id_type=MESH,
            ).start()
            return c

        lax.fori_loop(1, nt, send, 0)

    def all_tiles(source, target, sem):
        many = (nt - 1) * cap
        return pltpu.make_async_remote_copy(
            src_ref=source.at[pl.ds(0, many)],
            dst_ref=target.at[pl.ds(0, many)],
            send_sem=sem.at[0],
            recv_sem=sem.at[1],
            device_id={"tile": lax.rem(me + 1, nt)},
            device_id_type=MESH,
        )

    for step in range(1, nd):
        across_depth(lambda q: lists_rx.at[my], lists_rx.at[my], lists_send, lists_recv, step).start()
    scatter_tiles(geo_tx, geo_rx, geo_sem)
    scatter_tiles(feat_tx, feat_rx, feat_sem)

    for step in range(1, nd):
        arrived_depth(lambda q: lists_rx.at[q], lists_send, lists_recv, step).wait_recv()
    to_scalar = pltpu.make_async_copy(lists_rx, lists_sm, local_sem.at[1])
    to_scalar.start()
    slot_of_row = iota((128, 128), 0)
    lane = iota((128, 128), 1)
    found = jnp.zeros((128, 128), I32)
    for q in range(nd):
        row = jnp.broadcast_to(lists_rx[q, 0:1, :], (128, 128))
        hit = (row == slot_of_row) & (lane < 32)
        found = found + jnp.where(hit, lane + 32 * q, 0)
    for shift in (64, 32, 16, 8, 4, 2, 1):
        found = found + pltpu.roll(found, shift, 1)
    inv_vec[...] = jnp.transpose(found)[0:8]
    to_scalar.wait()
    inv_copy = pltpu.make_async_copy(inv_vec, inv_sm, local_sem.at[2])
    inv_copy.start()

    def within(index):
        return jnp.clip(index, 0, slots - 1)

    def slot_at(par, g, k):
        return within(lists_sm[g // 2, 0, par * 16 + (g % 2) * 8 + k])

    def live_at(tile, g):
        return lists_sm[g // 2, 0, 64 + tile * 2 + g % 2]

    all_tiles(geo_tx, geo_rx, geo_sem).wait_recv()

    def sort_geo(at, c):
        for k in range(8):
            rows = geo_rx[slot_at(at // 8, at % 8, k)]
            group = at * 2 + k // 4
            for r in range(2):
                geo_part[r, k % 4, pl.ds(group, 1), :] = rows[r : r + 1, :]
        return c

    lax.fori_loop(0, 16, sort_geo, 0)
    lane_part = iota((32, 128), 1) // 32
    for p in range(6):
        r, m = p // 4, p % 4
        total = jnp.zeros((32, 128), F32)
        for i in range(4):
            shift = (32 * (i - m)) % 128
            part = geo_part[r, i]
            moved = pltpu.roll(part, shift, 1) if shift else part
            total = jnp.where(lane_part == i, moved, total)
        geo[p] = total

    row_in = iota((256, 128), 0) % 128
    lane_out = iota((256, 128), 1)
    same_block = row_in // 32 == lane_out // 32
    before_mat = ones_where(same_block & (row_in < lane_out))
    after_mat = ones_where(same_block & (row_in > lane_out))
    place_key = lane_out - row_in // 32
    column = iota((16, 128), 0).astype(F32) + 0.5
    entry_lane = iota((16, 128), 1) // 32

    def placing(base):
        return ones_where(place_key == base)

    def row_of(p, group):
        return jnp.broadcast_to(geo[p, pl.ds(group, 1), :], (16, 128))

    def origin(tile):
        return 16.0 * tile_ids[tile].astype(F32)

    def joined(pieces):
        return jnp.concatenate(pieces, axis=0)

    in_lane = iota((128, 256), 0)
    in_entry = in_lane % 64
    in_high = in_lane // 64
    out_entry = iota((128, 256), 1) // 32

    def offset_mat(high, g, later_ones):
        want = out_entry + g * 8
        key = jnp.where(in_high == high, in_entry, -1000 if later_ones else 1000)
        strict = key > want if later_ones else key < want
        pair = jnp.concatenate([ones_where(strict), ones_where(key == want)], axis=0)
        return jnp.concatenate([pair, pair], axis=0)

    def offsets_from(buffer, par, later_ones):
        total = buffer[par, 0] + buffer[par, 1] + buffer[par, 2] + buffer[par, 3]
        partial = jnp.zeros((256, 128), F32)
        for q in range(nd):
            counts = my < q if later_ones else my > q
            partial = partial + jnp.where(counts, 1.0, 0.0) * buffer[par, q]
        total_high, total_low = split_two(total)
        part_high, part_low = split_two(partial)
        offs[...] = jnp.concatenate([total_high, part_high, total_low, part_low], axis=1)

    for par in range(2):

        def alpha_step(g, c, par=par):
            for h in range(2):
                group = (par * 8 + g) * 2 + h
                mean_x, mean_y = row_of(0, group), row_of(1, group)
                half_a = -0.5 * row_of(2, group)
                minus_b = -row_of(3, group)
                half_c = -0.5 * row_of(4, group)
                opacity = row_of(5, group)
                for high in range(2):
                    tile = high * 2 + par
                    dx = column - (mean_x - origin(tile))
                    alive = entry_lane + h * 4 < live_at(tile, g)
                    ax = jnp.where(alive, half_a * dx * dx, -1e30)
                    highs, lows = [], []
                    for py in range(16):
                        dy = (py + 0.5) - mean_y
                        power = dx * (minus_b * dy) + (ax + half_c * dy * dy)
                        falloff = jnp.exp(power)
                        fall[tile, g * 2 + h, pl.ds(py * 16, 16), :] = falloff
                        log_keep = jnp.log(1.0 - opacity * falloff)
                        top, rest = split_two(log_keep)
                        highs.append(top)
                        lows.append(rest)
                    both = jnp.concatenate([joined(highs), joined(lows)], axis=1)
                    right = jnp.concatenate(
                        [before_mat, placing(high * 64 + g * 8 + h * 4)], axis=1
                    )
                    sums = jnp.dot(both, right, preferred_element_type=F32)
                    chain[tile, g * 2 + h] = sums[:, :128]
                    light_rx[par, my] += sums[:, 128:]
            return c

        lax.fori_loop(0, 8, alpha_step, 0)
        for step in range(1, nd):
            across_depth(
                lambda q: light_rx.at[par, my],
                light_rx.at[par, my],
                light_send.at[par],
                light_recv.at[par],
                step,
            ).start()

    inv_copy.wait()

    for par in range(2):
        for step in range(1, nd):
            arrived_depth(
                lambda q: light_rx.at[par, q], light_send.at[par], light_recv.at[par], step
            ).wait_recv()
        offsets_from(light_rx, par, False)

        def weight_step(g, c, par=par):
            grad = jnp.zeros((256, 128), F32)
            for high in range(2):
                tile = high * 2 + par
                ahead = jnp.dot(
                    offs[...], offset_mat(high, g, False), preferred_element_type=F32
                )
                halves = []
                for h in range(2):
                    group = (par * 8 + g) * 2 + h
                    opacity = jnp.broadcast_to(geo[5, pl.ds(group, 1), :], (256, 128))
                    through = jnp.exp(
                        chain[tile, g * 2 + h] + ahead[:, h * 128 : (h + 1) * 128]
                    )
                    chain[tile, g * 2 + h] = through
                    halves.append((through * (opacity * fall[tile, g * 2 + h])).astype(BF16))
                weight = jnp.concatenate(halves, axis=1)
                weights[tile, g] = weight
                grad = grad + lax.dot_general(
                    weight, cot[tile], (((0,), (0,)), ((), ())), preferred_element_type=F32
                )
            at = (g // 2) * 4 + par * 2 + g % 2
            grad_list[pl.ds(pl.multiple_of(at * 8, 8), 8)] = grad.astype(BF16).reshape(8, 32, 128)
            return c

        lax.fori_loop(0, 8, weight_step, 0)

    def back_feat(k, c):
        grad_tx[k] = grad_list[within(inv_sm[0, k])]
        return c

    lax.fori_loop(0, slots, back_feat, 0, unroll=8)
    keep_own = pltpu.make_async_copy(
        grad_tx.at[pl.ds(mine, cap)], grad_rx.at[pl.ds(mine, cap)], local_sem.at[3]
    )
    keep_own.start()
    all_tiles(feat_tx, feat_rx, feat_sem).wait_recv()
    scatter_tiles(grad_tx, grad_rx, grad_sem)

    def sort_feat(at, c):
        for k in range(8):
            feat_list[at, pl.ds(k * 32, 32), :] = feat_rx[slot_at(at // 8, at % 8, k)]
        return c

    lax.fori_loop(0, 16, sort_feat, 0)

    for par in range(2):

        def carry_step(g, c, par=par):
            feat = feat_list[par * 8 + g]
            for high in range(2):
                tile = high * 2 + par
                image_part[tile] += jnp.dot(weights[tile, g], feat, preferred_element_type=F32)
                dots = lax.dot_general(
                    cot[tile], feat, (((1,), (1,)), ((), ())), preferred_element_type=F32
                )
                for h in range(2):
                    group = (par * 8 + g) * 2 + h
                    opacity = jnp.broadcast_to(geo[5, pl.ds(group, 1), :], (256, 128))
                    direct = dots[:, h * 128 : (h + 1) * 128] * chain[tile, g * 2 + h]
                    chain[tile, g * 2 + h] = direct
                    carried = direct * (opacity * fall[tile, g * 2 + h])
                    top, rest = split_two(carried)
                    both = jnp.concatenate([top, rest], axis=1)
                    right = jnp.concatenate(
                        [after_mat, placing(high * 64 + g * 8 + h * 4)], axis=1
                    )
                    sums = jnp.dot(both, right, preferred_element_type=F32)
                    later[tile, g * 2 + h] = sums[:, :128]
                    carry_rx[par, my] += sums[:, 128:]
            return c

        lax.fori_loop(0, 8, carry_step, 0)
        for step in range(1, nd):
            across_depth(
                lambda q: carry_rx.at[par, my],
                carry_rx.at[par, my],
                carry_send.at[par],
                carry_recv.at[par],
                step,
            ).start()
    for step in range(1, nd):
        across_depth(
            lambda q: image_part.at[:, pl.ds(pl.multiple_of(q * 64, 64), 64), :],
            image_rx.at[my],
            image_send,
            image_recv,
            step,
        ).start()

    for par in range(2):
        for step in range(1, nd):
            arrived_depth(
                lambda q: carry_rx.at[par, q], carry_send.at[par], carry_recv.at[par], step
            ).wait_recv()
        offsets_from(carry_rx, par, True)

        def shape_step(g, c, par=par):
            behind = [
                jnp.dot(offs[...], offset_mat(high, g, True), preferred_element_type=F32)
                for high in range(2)
            ]
            for h in range(2):
                group = (par * 8 + g) * 2 + h
                mean_x, mean_y = row_of(0, group), row_of(1, group)
                opacity = row_of(5, group)
                moments = [jnp.zeros((16, 128), F32) for _ in range(6)]
                for high in range(2):
                    tile = high * 2 + par
                    dx = column - (mean_x - origin(tile))
                    flat = jnp.zeros((16, 128), F32)
                    tilt = jnp.zeros((16, 128), F32)
                    bend = jnp.zeros((16, 128), F32)
                    for py in range(16):
                        rows = pl.ds(py * 16, 16)
                        dy = (py + 0.5) - mean_y
                        falloff = fall[tile, g * 2 + h, rows, :]
                        after = (
                            later[tile, g * 2 + h, rows, :]
                            + behind[high][py * 16 : py * 16 + 16, h * 128 : (h + 1) * 128]
                        )
                        alpha_grad = chain[tile, g * 2 + h, rows, :] - after / (
                            1.0 - opacity * falloff
                        )
                        term = alpha_grad * falloff
                        term_y = term * dy
                        flat = flat + term
                        tilt = tilt + term_y
                        bend = bend + term_y * dy
                    flat_x = flat * dx
                    adds = [flat, flat_x, tilt, flat_x * dx, tilt * dx, bend]
                    moments = [a + b for a, b in zip(moments, adds)]
                one, sx, sy, sxx, sxy, syy = [
                    jnp.sum(m, axis=0, keepdims=True) for m in moments
                ]
                conic_a, conic_b, conic_c, opac = [
                    geo[p, pl.ds(group, 1), :] for p in (2, 3, 4, 5)
                ]
                ggeo[0, pl.ds(group, 1), :] = opac * (conic_a * sx + conic_b * sy)
                ggeo[1, pl.ds(group, 1), :] = opac * (conic_b * sx + conic_c * sy)
                ggeo[2, pl.ds(group, 1), :] = -0.5 * opac * sxx
                ggeo[3, pl.ds(group, 1), :] = -opac * sxy
                ggeo[4, pl.ds(group, 1), :] = -0.5 * opac * syy
                ggeo[5, pl.ds(group, 1), :] = one
            return c

        lax.fori_loop(0, 8, shape_step, 0)

    for i in range(4):
        for r in range(2):
            total = jnp.zeros((32, 128), F32)
            for m in range(4 if r == 0 else 2):
                shift = (32 * (m - i)) % 128
                part = ggeo[4 * r + m]
                moved = pltpu.roll(part, shift, 1) if shift else part
                total = jnp.where(lane_part == m, moved, total)
            ggeo_list[r, i] = total

    def back_geo(k, c):
        at = within(inv_sm[0, k])
        g = (at // 32) * 2 + (at // 8) % 2
        group = (((at // 16) % 2) * 8 + g) * 2 + (at % 8) // 4
        first = ggeo_list[0, at % 4, pl.ds(group, 1), :]
        second = ggeo_list[1, at % 4, pl.ds(group, 1), :]
        ggeo_tx[k] = jnp.concatenate([first, second], axis=0)
        return c

    lax.fori_loop(0, slots, back_geo, 0, unroll=8)
    keep_geo = pltpu.make_async_copy(
        ggeo_tx.at[pl.ds(mine, cap)], ggeo_rx.at[pl.ds(mine, cap)], local_sem.at[4]
    )
    keep_geo.start()
    scatter_tiles(ggeo_tx, ggeo_rx, ggeo_sem)

    image = image_part[:, pl.ds(pl.multiple_of(my * 64, 64), 64), :]
    for step in range(1, nd):
        arrived_depth(lambda q: image_rx.at[q], image_send, image_recv, step).wait_recv()
    for step in range(1, nd):
        image = image + image_rx[lax.rem(my + step, nd)]
    image_out[...] = image.astype(BF16)

    for step in range(1, nd):
        arrived_depth(lambda q: lists_rx.at[q], lists_send, lists_recv, step).wait_send()
        arrived_depth(lambda q: image_rx.at[q], image_send, image_recv, step).wait_send()
        for par in range(2):
            arrived_depth(
                lambda q: light_rx.at[par, q], light_send.at[par], light_recv.at[par], step
            ).wait_send()
            arrived_depth(
                lambda q: carry_rx.at[par, q], carry_send.at[par], carry_recv.at[par], step
            ).wait_send()
    all_tiles(geo_tx, geo_rx, geo_sem).wait_send()
    all_tiles(feat_tx, feat_rx, feat_sem).wait_send()
    keep_own.wait()
    keep_geo.wait()
    all_tiles(grad_tx, grad_rx, grad_sem).wait()
    all_tiles(ggeo_tx, ggeo_rx, ggeo_sem).wait()


def owner_kernel(picked, grad_rx, ggeo_rx, grad_out, ggeo_out):
    def put(k, c):
        at = picked[k]
        grad_out[at] = grad_rx[k].astype(F32)
        ggeo_out[at] = ggeo_rx[k]
        return c

    lax.fori_loop(0, grad_rx.shape[0], put, 0, unroll=8)


def local(features, geometry, send_lists, tile_ids, tile_lists, live_counts, cotangent):
    nt, nd = lax.axis_size("tile"), lax.axis_size("depth")
    my = lax.axis_index("depth")
    cap = send_lists.shape[2]
    slots = nt * cap
    blocks = features.shape[0]
    picked = send_lists.reshape(slots)
    quarter = lax.dynamic_slice_in_dim(geometry, my * 32, 32, 2)
    geo_own = jnp.pad(quarter, ((0, 0), (0, 2), (0, 0))).reshape(blocks, 2, 128)
    row = jnp.concatenate(
        [tile_lists.reshape(64), live_counts.reshape(8), jnp.zeros((56,), I32)]
    )
    lists_own = jnp.broadcast_to(row[None, :], (8, 128))

    vmem = pl.BlockSpec(memory_space=pltpu.VMEM)
    smem = pl.BlockSpec(memory_space=pltpu.SMEM)
    hbm = pl.BlockSpec(memory_space=pl.ANY)
    dma = pltpu.SemaphoreType.DMA
    image_out, grad_rx, ggeo_rx = pl.pallas_call(
        functools.partial(splat_kernel, nt, nd, cap),
        out_shape=(
            jax.ShapeDtypeStruct((4, 64, 128), BF16),
            jax.ShapeDtypeStruct((slots, 32, 128), BF16),
            jax.ShapeDtypeStruct((slots, 2, 128), F32),
        ),
        in_specs=[hbm, vmem, vmem, smem, smem, vmem],
        out_specs=(vmem, hbm, hbm),
        scratch_shapes=[
            pltpu.VMEM((blocks, 32, 128), BF16),
            pltpu.VMEM((slots, 32, 128), BF16),
            pltpu.VMEM((slots, 32, 128), BF16),
            pltpu.VMEM((16, 256, 128), BF16),
            pltpu.VMEM((slots, 2, 128), F32),
            pltpu.VMEM((slots, 2, 128), F32),
            pltpu.VMEM((nd, 8, 128), I32),
            pltpu.VMEM((8, 128), I32),
            pltpu.SMEM((nd, 8, 128), I32),
            pltpu.SMEM((8, 128), I32),
            pltpu.VMEM((2, 4, 32, 128), F32),
            pltpu.VMEM((6, 32, 128), F32),
            pltpu.VMEM((4, 16, 256, 128), F32),
            pltpu.VMEM((4, 16, 256, 128), F32),
            pltpu.VMEM((4, 16, 256, 128), F32),
            pltpu.VMEM((4, 8, 256, 256), BF16),
            pltpu.VMEM((2, nd, 256, 128), F32),
            pltpu.VMEM((2, nd, 256, 128), F32),
            pltpu.VMEM((256, 512), BF16),
            pltpu.VMEM((slots, 32, 128), BF16),
            pltpu.VMEM((slots, 32, 128), BF16),
            pltpu.VMEM((6, 32, 128), F32),
            pltpu.VMEM((2, 4, 32, 128), F32),
            pltpu.VMEM((slots, 2, 128), F32),
            pltpu.VMEM((4, 256, 128), F32),
            pltpu.VMEM((nd, 4, 64, 128), F32),
            dma((5,)),
            dma((2,)),
            dma((2,)),
            dma((2,)),
            dma((2,)),
            dma((nd,)),
            dma((nd,)),
            dma((2, nd)),
            dma((2, nd)),
            dma((2, nd)),
            dma((2, nd)),
            dma((nd,)),
            dma((nd,)),
        ],
        compiler_params=pltpu.CompilerParams(
            collective_id=0, has_side_effects=True, vmem_limit_bytes=62 * 1024 * 1024
        ),
        name="splat",
    )(features, geo_own, lists_own, picked, tile_ids, cotangent)

    feature_grads, ggeo = pl.pallas_call(
        owner_kernel,
        out_shape=(
            jax.ShapeDtypeStruct((blocks, 32, 128), F32),
            jax.ShapeDtypeStruct((blocks, 2, 128), F32),
        ),
        in_specs=[smem, vmem, vmem],
        out_specs=(vmem, vmem),
        name="owner",
    )(picked, grad_rx, ggeo_rx)
    geometry_grads = ggeo.reshape(blocks, 8, 32)[:, :6]
    return image_out, feature_grads, geometry_grads


def solution(mesh):
    placed = (
        P("tile", None, None),
        P("tile", None, None),
        P("tile", None, None),
        P("tile"),
        P("tile", "depth", None),
        P("tile", "depth"),
        P("tile", None, None),
    )
    return jax.shard_map(
        local,
        mesh=mesh,
        in_specs=placed,
        out_specs=(P("tile", "depth", None), P("tile", "depth", None), P("tile", None, "depth")),
        check_vma=False,
    )
```

time: 456 us -> 91.9 us (0.20)
  waiting for transfers between devices: 115 us -> 0 us
  matrix products: 104 us -> 0 us
  Pallas kernels: 0 us -> 83 us
  local copies, waits for them, and re-layouts: 90.1 us -> 7.89 us
  blocking collectives: 60 us -> 0 us
  other arithmetic: 35.8 us -> 0.08 us
  starting transfers between devices: 33.7 us -> 0 us
  between operations: 14.1 us -> 0.68 us
    dot_general x52 -> x0, matrix products: 104 us -> none  [the longest x24 66.7 us: along_gauss(): jnp.dot(flat, matrix, precision=precise, preferred_element_type=jnp.float32)]
    pallas_call x0 -> x2, Pallas kernels: none -> 83 us  [the longest x1 80.1 us: local(): pl.pallas_call(functools.partial(splat_kernel, nt, nd, cap), out_shape=(j...]
    gather x34 -> x0, local copies, waits for them, and re-layouts: 72 us -> none  [the longest x8 22.3 us: forward_step(): block_feat = jnp.take(pool_feat, slot_ids, axis=0)]
    reduce_scatter x2 -> x0, waiting for transfers between devices: 50.8 us -> none  [the longest x1 39.6 us: local(): lax.psum_scatter(pool_dfeat.reshape(pool_size, gauss_count, feat_count).a...]
    all_to_all x1 -> x0, blocking collectives: 41.6 us -> none  [local(): lax.all_to_all(sent_feat, 'tile', split_axis=0, concat_axis=0, tiled=True)]
    all_to_all x4 -> x0, waiting for transfers between devices: 40.3 us -> none  [the longest x1 26.4 us: local(): lax.all_to_all(part_dfeat.reshape(tile_count, capacity, quarter, feat_cou...]
    all_to_all x4 -> x0, starting transfers between devices: 33.6 us -> none  [the longest x1 13 us: local(): lax.all_to_all(part_dshape.reshape(tile_count, capacity, 6, quarter).asty...]
    reduce_sum x18 -> x0, other arithmetic: 30.5 us -> none  [the longest x8 20.9 us: backward_step(): jnp.sum(alpha_grad * falloff * live_mask[:, None, None], axis=1)]
  transfers between devices with their start and end apart: 7 -> 0, of which waited for: 5 -> 0; matrix products, arithmetic and copies ran while one was open for 5% -> 0% of each run, Pallas kernels for 0% -> 0%
where the time goes in v1:
time: 91.9 us; the launch traced here: 91.6 us
  Pallas kernels  83 us (90%)
  local copies, waits for them, and re-layouts  7.89 us (9%)
    pallas_call x1, Pallas kernels, local(): pl.pallas_call(functools.partial(splat_kernel, nt, nd, cap), out_shape=(j...  80.1 us
    unnamed x6, local copies, waits for them, and re-layouts  3.16 us
    pallas_call x1, Pallas kernels, local(): pl.pallas_call(owner_kernel, out_shape=(jax.ShapeDtypeStruct((blocks, 32,...  2.9 us

profile of v1, /device:TPU:1, one launch (start us, length us, event | category | flops | bytes accessed | tf_op | source)
XLA Modules:
  0.0 91.6 jit_solution(3652070944624633509)
XLA Ops:
  0.6 0.0 copy-start
  0.6 0.8 reshape.23
  1.5 0.8 copy.15
  2.2 0.1 reshape.24
  2.3 0.1 pad_add_fusion
  2.4 0.6 broadcast_in_dim.10.lists_own
  3.0 0.8 copy.16
  3.8 0.7 reshape.25.picked
  4.4 0.0 copy-done
  4.4 0.2 constant_dynamic-slice_fusion
  4.6 0.1 copy.19
  4.8 0.8 copy.17.geo_own
  5.5 80.1 %splat.1 = (bf16[4,64,128]{2,1,0:T(8,128)(2,1)}, bf16[128,32,128]{2,1,0:T(8,128)(2,1)}, f32[128,2,128]{2,1,0:T(2,128)}) custom-call(bf16[128,128,128]{2,1,0:T(8,128)(2,1)} %features.1, f32[128,2,128]{2,1,0:T(2,128)} %copy.17.geo_own, s32[8,128]{1,0:T(8,128)} %broadcast_in_dim.10.lists_own, s32[128]{0:T(128)} %reshape.25.picked, s32[4]{0:T(128)} %tile_ids.1, ...), custom_call_target="tpu_custom_call" | custom-call | tf_op jit(solution)/shard_map/splat/pallas_call | solution.py:555
  85.6 2.9 %owner.1 = (f32[128,32,128]{2,1,0:T(8,128)}, f32[128,2,128]{2,1,0:T(2,128)}) custom-call(s32[128]{0:T(128)} %reshape.25.picked, bf16[128,32,128]{2,1,0:T(8,128)(2,1)} %get-tuple-element.9.grad_rx, f32[128,2,128]{2,1,0:T(2,128)} %get-tuple-element.10.ggeo_rx), custom_call_target="tpu_custom_call" | custom-call | tf_op jit(solution)/shard_map/owner/pallas_call | solution.py:611
  88.5 1.0 %copy.18 = f32[128,2,128]{0,2,1:T(8,128)S(1)} copy(f32[128,2,128]{2,1,0:T(2,128)} %get-tuple-element.12) | data formatting | bytes 262144 | tf_op jit(solution)/shard_map/owner/pallas_call | solution.py:611
  89.5 0.7 slice.4
  90.1 1.5 %copy.21 = bf16[4,64,128]{2,1,0:T(8,128)(2,1)} copy(bf16[4,64,128]{2,1,0:T(8,128)(2,1)} %get-tuple-element.16) | data formatting | bytes 131072
  (2 shorter events, 0.0 us)
Async XLA Ops:
  0.6 3.8 %copy-start = (f32[128,6,128]{2,0,1:T(8,128)S(1)}, f32[128,6,128]{2,0,1:T(8,128)}, u32[]{:S(2)}) copy-start(f32[128,6,128]{2,0,1:T(8,128)} %param.8) | copy-start | bytes 1179652

commit v2 on v1

v2 whole, which is shorter than its diff:
```python
import functools

import jax
import jax.numpy as jnp
from jax import lax
from jax.experimental import pallas as pl
from jax.experimental.pallas import tpu as pltpu
from jax.sharding import PartitionSpec as P

MESH = pl.DeviceIdType.MESH
F32 = jnp.float32
BF16 = jnp.bfloat16
I32 = jnp.int32


def iota(shape, dim):
    return lax.broadcasted_iota(I32, shape, dim)


def ones_where(mask):
    return jnp.where(mask, 1.0, 0.0).astype(BF16)


def split_two(value):
    high = value.astype(BF16)
    low = (value - high.astype(F32)).astype(BF16)
    return high, low


def splat_kernel(
    nt,
    nd,
    cap,
    features,
    geometry,
    picked,
    tile_ids,
    tile_lists,
    live_counts,
    cotangent,
    image_out,
    grad_rx,
    ggeo_rx,
    own_feat,
    own_geo,
    feat_tx,
    feat_rx,
    feat_list,
    geo_rows,
    geo_tx,
    geo_rx,
    lists_rx,
    inv_vec,
    lists_sm,
    inv_sm,
    geo_part,
    geo,
    cot,
    place_mat,
    ahead_mat,
    behind_mat,
    fall,
    chain,
    later,
    weights,
    sums,
    light,
    carry,
    offs,
    grad_sum,
    grad_list,
    grad_tx,
    moment,
    ggeo_list,
    ggeo_tx,
    image_part,
    image_rx,
    local_sem,
    geo_sem,
    feat_sem,
    grad_sem,
    ggeo_sem,
    lists_send,
    lists_recv,
    light_send,
    light_recv,
    carry_send,
    carry_recv,
    image_send,
    image_recv,
):
    me = lax.axis_index("tile")
    my = lax.axis_index("depth")
    slots = nt * cap
    near = my + 1 - 2 * (my % 2)
    far = nd - 1 - my

    def greet(i, c):
        pl.semaphore_signal(
            barrier, inc=1, device_id={"tile": lax.rem(me + i, nt)}, device_id_type=MESH
        )
        return c

    barrier = pltpu.get_barrier_semaphore()
    lax.fori_loop(1, nt, greet, 0)
    for step in range(1, nd):
        pl.semaphore_signal(
            barrier, inc=1, device_id={"depth": lax.rem(my + step, nd)}, device_id_type=MESH
        )

    fetch_geo = pltpu.make_async_copy(geometry, own_geo, local_sem.at[0])
    fetch_geo.start()
    fetch_feat = pltpu.make_async_copy(
        features.at[:, pl.ds(pl.multiple_of(my * 32, 32), 32), :], own_feat, local_sem.at[1]
    )
    fetch_feat.start()
    fetch_cot = []
    for par in range(2):
        for ph in range(2):
            for high in range(2):
                copy = pltpu.make_async_copy(
                    cotangent.at[high * 2 + par, pl.ds(ph * 128, 128), :],
                    cot.at[par * 2 + ph, pl.ds(high * 128, 128), :],
                    local_sem.at[5 + par * 4 + ph * 2 + high],
                )
                copy.start()
                fetch_cot.append(copy)

    lane8 = iota((8, 128), 1)
    listed = jnp.zeros((8, 128), I32)
    for u in range(4):
        for g in range(2):
            for k in range(8):
                listed = jnp.where(lane8 == u * 16 + g * 8 + k, tile_lists[u, g, k], listed)
            listed = jnp.where(lane8 == 64 + u * 2 + g, live_counts[g, u], listed)
    lists_rx[my] = listed

    fetch_geo.wait()
    lane_group = iota((slots, 128), 1) // 32
    for r in range(2):
        total = jnp.zeros((slots, 128), F32)
        for m in range(4 if r == 0 else 2):
            shift = lax.rem(32 * m + 128 - 32 * my, 128)
            total = jnp.where(lane_group == m, pltpu.roll(own_geo[4 * r + m], shift, 1), total)
        geo_rows[r] = total

    def pick_geo(t, c):
        for j in range(cap):
            at = picked[j, t]
            first = geo_rows[0, pl.ds(at, 1), :]
            second = geo_rows[1, pl.ds(at, 1), :]
            geo_tx[t * cap + j] = jnp.concatenate([first, second], axis=0)
        return c

    lax.fori_loop(0, nt, pick_geo, 0, unroll=4)
    mine = pl.multiple_of(me * cap, cap)
    geo_rx[pl.ds(mine, cap)] = geo_tx[pl.ds(mine, cap)]

    def across_depth(source, target, send, recv, peer):
        return pltpu.make_async_remote_copy(
            src_ref=source,
            dst_ref=target,
            send_sem=send,
            recv_sem=recv,
            device_id={"depth": peer},
            device_id_type=MESH,
        )

    def scatter_tiles(source, target, sem):
        def send(i, c):
            peer = lax.rem(me + i, nt)
            there = pl.multiple_of(peer * cap, cap)
            pltpu.make_async_remote_copy(
                src_ref=source.at[pl.ds(there, cap)],
                dst_ref=target.at[pl.ds(mine, cap)],
                send_sem=sem.at[0],
                recv_sem=sem.at[1],
                device_id={"tile": peer},
                device_id_type=MESH,
            ).start()
            return c

        lax.fori_loop(1, nt, send, 0)

    def all_tiles(source, target, sem):
        many = (nt - 1) * cap
        return pltpu.make_async_remote_copy(
            src_ref=source.at[pl.ds(0, many)],
            dst_ref=target.at[pl.ds(0, many)],
            send_sem=sem.at[0],
            recv_sem=sem.at[1],
            device_id={"tile": lax.rem(me + 1, nt)},
            device_id_type=MESH,
        )

    pl.semaphore_wait(barrier, nt - 1 + nd - 1)
    for step in range(1, nd):
        peer = lax.rem(my + step, nd)
        across_depth(
            lists_rx.at[my], lists_rx.at[my], lists_send.at[peer], lists_recv.at[my], peer
        ).start()
    scatter_tiles(geo_tx, geo_rx, geo_sem)

    fetch_feat.wait()

    def pick_feat(t, c):
        for j in range(cap):
            feat_tx[t * cap + j] = own_feat[picked[j, t]]
        return c

    lax.fori_loop(0, nt, pick_feat, 0, unroll=4)
    feat_rx[pl.ds(mine, cap)] = feat_tx[pl.ds(mine, cap)]
    scatter_tiles(feat_tx, feat_rx, feat_sem)

    row_in = iota((256, 128), 0) % 128
    lane_out = iota((256, 128), 1)
    same_block = row_in // 32 == lane_out // 32
    before_mat = ones_where(same_block & (row_in < lane_out))
    after_mat = ones_where(same_block & (row_in > lane_out))
    place_key = lane_out - row_in // 32
    in_entry = iota((64, 256), 0)
    out_entry = iota((64, 256), 1) // 32

    def build(g, c):
        for h in range(2):
            place_mat[g * 2 + h] = ones_where(place_key == g * 8 + h * 4)
        want = out_entry + g * 8
        equal = ones_where(in_entry == want)
        less = ones_where(in_entry < want)
        more = ones_where(in_entry > want)
        ahead_mat[g] = jnp.concatenate([less, equal, less, equal], axis=0)
        behind_mat[g] = jnp.concatenate([more, equal, more, equal], axis=0)
        return c

    lax.fori_loop(0, 8, build, 0)

    for step in range(1, nd):
        other = lax.rem(my + step, nd)
        across_depth(
            lists_rx.at[other], lists_rx.at[other], lists_send.at[other], lists_recv.at[other], other
        ).wait_recv()
    to_scalar = pltpu.make_async_copy(lists_rx, lists_sm, local_sem.at[2])
    to_scalar.start()
    slot_of_row = iota((128, 128), 0)
    lane = iota((128, 128), 1)
    found = jnp.zeros((128, 128), I32)
    for q in range(nd):
        row = jnp.broadcast_to(lists_rx[q, 0:1, :], (128, 128))
        hit = (row == slot_of_row) & (lane < 32)
        found = found + jnp.where(hit, lane + 32 * q, 0)
    for shift in (64, 32, 16, 8, 4, 2, 1):
        found = found + pltpu.roll(found, shift, 1)
    inv_vec[...] = jnp.transpose(found)[0:8]
    to_scalar.wait()
    inv_copy = pltpu.make_async_copy(inv_vec, inv_sm, local_sem.at[3])
    inv_copy.start()

    def within(index):
        return jnp.clip(index, 0, slots - 1)

    def slot_at(par, g, k):
        return within(lists_sm[g // 2, 0, par * 16 + (g % 2) * 8 + k])

    def live_at(tile, g):
        return lists_sm[g // 2, 0, 64 + tile * 2 + g % 2]

    all_tiles(geo_tx, geo_rx, geo_sem).wait_recv()

    def sort_geo(at, c):
        for k in range(8):
            rows = geo_rx[slot_at(at // 8, at % 8, k)]
            group = at * 2 + k // 4
            for r in range(2):
                geo_part[r, k % 4, pl.ds(group, 1), :] = rows[r : r + 1, :]
        return c

    lax.fori_loop(0, 16, sort_geo, 0)
    lane_part = iota((32, 128), 1) // 32
    for p in range(6):
        r, m = p // 4, p % 4
        total = jnp.zeros((32, 128), F32)
        for i in range(4):
            shift = (32 * (i - m)) % 128
            part = geo_part[r, i]
            moved = pltpu.roll(part, shift, 1) if shift else part
            total = jnp.where(lane_part == i, moved, total)
        geo[p] = total

    column = iota((16, 128), 0).astype(F32) + 0.5
    entry_lane = iota((16, 128), 1) // 32
    left = iota((128, 128), 1) < 64

    def row_of(p, group):
        return jnp.broadcast_to(geo[p, pl.ds(group, 1), :], (16, 128))

    def origin(tile):
        return 16.0 * tile_ids[tile].astype(F32)

    def start_near(buffer, send, recv, chunk):
        whole = sums[...]
        buffer[chunk, 0] = jnp.where(left, whole[:128], pltpu.roll(whole[128:], 64, 1))
        across_depth(
            buffer.at[chunk, 0], buffer.at[chunk, 1], send.at[0, chunk], recv.at[0, chunk], near
        ).start()

    def start_far(buffer, send, recv, chunk):
        across_depth(
            buffer.at[chunk, 1], buffer.at[chunk, 1], send.at[0, chunk], recv.at[0, chunk], near
        ).wait_recv()
        buffer[chunk, 3] = buffer[chunk, 0] + buffer[chunk, 1]
        across_depth(
            buffer.at[chunk, 3], buffer.at[chunk, 2], send.at[1, chunk], recv.at[1, chunk], far
        ).start()

    def offsets_from(buffer, send, recv, chunk, use_near, use_far):
        across_depth(
            buffer.at[chunk, 2], buffer.at[chunk, 2], send.at[1, chunk], recv.at[1, chunk], far
        ).wait_recv()
        total = buffer[chunk, 3] + buffer[chunk, 2]
        same = use_near * buffer[chunk, 1] + use_far * buffer[chunk, 2]
        for high in range(2):
            if high == 0:
                both = jnp.where(left, total, pltpu.roll(same, 64, 1))
            else:
                both = jnp.where(left, pltpu.roll(total, 64, 1), same)
            top, rest = split_two(both)
            offs[pl.ds(high * 128, 128), :] = jnp.concatenate([top, rest], axis=1)

    odd = jnp.where(my % 2 == 1, 1.0, 0.0)
    upper = jnp.where(my >= 2, 1.0, 0.0)

    for chunk in range(4):
        par, ph = chunk // 2, chunk % 2
        sums[...] = jnp.zeros((256, 128), F32)

        def alpha_step(g, c, par=par, ph=ph, chunk=chunk):
            for h in range(2):
                group = (par * 8 + g) * 2 + h
                mean_x, mean_y = row_of(0, group), row_of(1, group)
                half_a = -0.5 * row_of(2, group)
                minus_b = -row_of(3, group)
                half_c = -0.5 * row_of(4, group)
                opacity = row_of(5, group)
                highs, lows = [], []
                for high in range(2):
                    tile = high * 2 + par
                    dx = column - (mean_x - origin(tile))
                    alive = entry_lane + h * 4 < live_at(tile, g)
                    ax = jnp.where(alive, half_a * dx * dx, -1e30)
                    for py in range(8):
                        dy = (py + ph * 8 + 0.5) - mean_y
                        power = dx * (minus_b * dy) + (ax + half_c * dy * dy)
                        falloff = jnp.exp(power)
                        fall[chunk, g * 2 + h, pl.ds(high * 128 + py * 16, 16), :] = falloff
                        top, rest = split_two(jnp.log(1.0 - opacity * falloff))
                        highs.append(top)
                        lows.append(rest)
                both = jnp.concatenate(
                    [jnp.concatenate(highs, axis=0), jnp.concatenate(lows, axis=0)], axis=1
                )
                right = jnp.concatenate([before_mat, place_mat[g * 2 + h]], axis=1)
                result = jnp.dot(both, right, preferred_element_type=F32)
                chain[chunk, g * 2 + h] = result[:, :128]
                sums[...] += result[:, 128:]
            return c

        lax.fori_loop(0, 8, alpha_step, 0)
        start_near(light, light_send, light_recv, chunk)
        if chunk:
            start_far(light, light_send, light_recv, chunk - 1)

    for copy in fetch_cot:
        copy.wait()
    inv_copy.wait()

    for chunk in range(4):
        par, ph = chunk // 2, chunk % 2
        if chunk == 1:
            start_far(light, light_send, light_recv, 3)
        offsets_from(light, light_send, light_recv, chunk, odd, upper)

        def weight_step(g, c, par=par, ph=ph, chunk=chunk):
            ahead = jnp.dot(offs[...], ahead_mat[g], preferred_element_type=F32)
            halves = []
            for h in range(2):
                group = (par * 8 + g) * 2 + h
                opacity = jnp.broadcast_to(geo[5, pl.ds(group, 1), :], (256, 128))
                through = jnp.exp(chain[chunk, g * 2 + h] + ahead[:, h * 128 : (h + 1) * 128])
                chain[chunk, g * 2 + h] = through
                halves.append((through * (opacity * fall[chunk, g * 2 + h])).astype(BF16))
            weight = jnp.concatenate(halves, axis=1)
            weights[chunk, g] = weight
            grad = lax.dot_general(
                weight, cot[chunk], (((0,), (0,)), ((), ())), preferred_element_type=F32
            )
            if ph == 0:
                grad_sum[g] = grad
            else:
                grad = grad + grad_sum[g]
                at = (g // 2) * 4 + par * 2 + g % 2
                grad_list[pl.ds(pl.multiple_of(at * 8, 8), 8)] = grad.astype(BF16).reshape(
                    8, 32, 128
                )
            return c

        lax.fori_loop(0, 8, weight_step, 0)

    def back_feat(k, c):
        grad_tx[k] = grad_list[within(inv_sm[0, k])]
        return c

    lax.fori_loop(0, slots, back_feat, 0, unroll=8)
    keep_own = pltpu.make_async_copy(
        grad_tx.at[pl.ds(mine, cap)], grad_rx.at[pl.ds(mine, cap)], local_sem.at[4]
    )
    keep_own.start()
    scatter_tiles(grad_tx, grad_rx, grad_sem)
    all_tiles(feat_tx, feat_rx, feat_sem).wait_recv()

    def sort_feat(at, c):
        for k in range(8):
            feat_list[at, pl.ds(k * 32, 32), :] = feat_rx[slot_at(at // 8, at % 8, k)]
        return c

    lax.fori_loop(0, 16, sort_feat, 0)
    image_part[...] = jnp.zeros(image_part.shape, F32)

    for chunk in range(4):
        par, ph = chunk // 2, chunk % 2
        sums[...] = jnp.zeros((256, 128), F32)

        def carry_step(g, c, par=par, ph=ph, chunk=chunk):
            feat = feat_list[par * 8 + g]
            shown = jnp.dot(weights[chunk, g], feat, preferred_element_type=F32)
            image_part[par, ph] += shown.reshape(2, 128, 128)
            dots = lax.dot_general(
                cot[chunk], feat, (((1,), (1,)), ((), ())), preferred_element_type=F32
            )
            for h in range(2):
                group = (par * 8 + g) * 2 + h
                opacity = jnp.broadcast_to(geo[5, pl.ds(group, 1), :], (256, 128))
                direct = dots[:, h * 128 : (h + 1) * 128] * chain[chunk, g * 2 + h]
                chain[chunk, g * 2 + h] = direct
                top, rest = split_two(direct * (opacity * fall[chunk, g * 2 + h]))
                both = jnp.concatenate([top, rest], axis=1)
                right = jnp.concatenate([after_mat, place_mat[g * 2 + h]], axis=1)
                result = jnp.dot(both, right, preferred_element_type=F32)
                later[chunk, g * 2 + h] = result[:, :128]
                sums[...] += result[:, 128:]
            return c

        lax.fori_loop(0, 8, carry_step, 0)
        start_near(carry, carry_send, carry_recv, chunk)
        if chunk:
            start_far(carry, carry_send, carry_recv, chunk - 1)

    for chunk in range(4):
        par, ph = chunk // 2, chunk % 2
        if chunk == 1:
            start_far(carry, carry_send, carry_recv, 3)
            for step in range(1, nd):
                peer = lax.rem(my + step, nd)
                across_depth(
                    image_part.at[
                        :, peer // 2, :, pl.ds(pl.multiple_of((peer % 2) * 64, 64), 64), :
                    ],
                    image_rx.at[my],
                    image_send.at[peer],
                    image_recv.at[my],
                    peer,
                ).start()
        offsets_from(carry, carry_send, carry_recv, chunk, 1.0 - odd, 1.0 - upper)

        def shape_step(g, c, par=par, ph=ph, chunk=chunk):
            behind = jnp.dot(offs[...], behind_mat[g], preferred_element_type=F32)
            for h in range(2):
                group = (par * 8 + g) * 2 + h
                mean_x, mean_y = row_of(0, group), row_of(1, group)
                opacity = row_of(5, group)
                parts = [jnp.zeros((16, 128), F32) for _ in range(6)]
                for high in range(2):
                    tile = high * 2 + par
                    dx = column - (mean_x - origin(tile))
                    flat = jnp.zeros((16, 128), F32)
                    tilt = jnp.zeros((16, 128), F32)
                    bend = jnp.zeros((16, 128), F32)
                    for py in range(8):
                        at = high * 128 + py * 16
                        rows = pl.ds(at, 16)
                        dy = (py + ph * 8 + 0.5) - mean_y
                        falloff = fall[chunk, g * 2 + h, rows, :]
                        after = (
                            later[chunk, g * 2 + h, rows, :]
                            + behind[at : at + 16, h * 128 : (h + 1) * 128]
                        )
                        alpha_grad = chain[chunk, g * 2 + h, rows, :] - after / (
                            1.0 - opacity * falloff
                        )
                        term = alpha_grad * falloff
                        term_y = term * dy
                        flat = flat + term
                        tilt = tilt + term_y
                        bend = bend + term_y * dy
                    flat_x = flat * dx
                    adds = [flat, flat_x, tilt, flat_x * dx, tilt * dx, bend]
                    parts = [a + b for a, b in zip(parts, adds)]
                for i, part in enumerate(parts):
                    folded = jnp.sum(part, axis=0, keepdims=True)
                    if ph:
                        folded = folded + moment[i, pl.ds(group, 1), :]
                    moment[i, pl.ds(group, 1), :] = folded
            return c

        lax.fori_loop(0, 8, shape_step, 0)

    one, sx, sy, sxx, sxy, syy = [moment[i] for i in range(6)]
    conic_a, conic_b, conic_c, opac = [geo[p] for p in (2, 3, 4, 5)]
    ggeo = [
        opac * (conic_a * sx + conic_b * sy),
        opac * (conic_b * sx + conic_c * sy),
        -0.5 * opac * sxx,
        -opac * sxy,
        -0.5 * opac * syy,
        one,
    ]
    for i in range(4):
        for r in range(2):
            total = jnp.zeros((32, 128), F32)
            for m in range(4 if r == 0 else 2):
                shift = (32 * (m - i)) % 128
                part = ggeo[4 * r + m]
                moved = pltpu.roll(part, shift, 1) if shift else part
                total = jnp.where(lane_part == m, moved, total)
            ggeo_list[r, i] = total

    def back_geo(k, c):
        at = within(inv_sm[0, k])
        g = (at // 32) * 2 + (at // 8) % 2
        group = (((at // 16) % 2) * 8 + g) * 2 + (at % 8) // 4
        first = ggeo_list[0, at % 4, pl.ds(group, 1), :]
        second = ggeo_list[1, at % 4, pl.ds(group, 1), :]
        ggeo_tx[k] = jnp.concatenate([first, second], axis=0)
        return c

    lax.fori_loop(0, slots, back_geo, 0, unroll=8)
    keep_geo = pltpu.make_async_copy(
        ggeo_tx.at[pl.ds(mine, cap)], ggeo_rx.at[pl.ds(mine, cap)], local_sem.at[13]
    )
    keep_geo.start()
    scatter_tiles(ggeo_tx, ggeo_rx, ggeo_sem)

    image = image_part[:, my // 2, :, pl.ds(pl.multiple_of((my % 2) * 64, 64), 64), :]
    for step in range(1, nd):
        other = lax.rem(my + step, nd)
        across_depth(
            image_rx.at[other], image_rx.at[other], image_send.at[other], image_recv.at[other], other
        ).wait_recv()
        image = image + image_rx[other]
    for par in range(2):
        for high in range(2):
            image_out[high * 2 + par] = image[par, high].astype(BF16)

    for step in range(1, nd):
        other = lax.rem(my + step, nd)
        across_depth(
            lists_rx.at[other], lists_rx.at[other], lists_send.at[other], lists_recv.at[other], other
        ).wait_send()
        across_depth(
            image_rx.at[other], image_rx.at[other], image_send.at[other], image_recv.at[other], other
        ).wait_send()
    for buffer, send, recv in ((light, light_send, light_recv), (carry, carry_send, carry_recv)):
        for chunk in range(4):
            across_depth(
                buffer.at[chunk, 0], buffer.at[chunk, 1], send.at[0, chunk], recv.at[0, chunk], near
            ).wait_send()
            across_depth(
                buffer.at[chunk, 3], buffer.at[chunk, 2], send.at[1, chunk], recv.at[1, chunk], far
            ).wait_send()
    all_tiles(geo_tx, geo_rx, geo_sem).wait_send()
    all_tiles(feat_tx, feat_rx, feat_sem).wait_send()
    keep_own.wait()
    keep_geo.wait()
    all_tiles(grad_tx, grad_rx, grad_sem).wait()
    all_tiles(ggeo_tx, ggeo_rx, ggeo_sem).wait()


def owner_kernel(picked, grad_rx, ggeo_rx, grad_out, ggeo_out, rows):
    cap, nt = picked.shape

    def put(t, c):
        for j in range(cap):
            k = t * cap + j
            at = picked[j, t]
            grad_out[at] = grad_rx[k].astype(F32)
            for r in range(2):
                rows[r, pl.ds(at, 1), :] = ggeo_rx[k, r : r + 1, :]
        return c

    lax.fori_loop(0, nt, put, 0, unroll=4)
    for r in range(2):
        turned = jnp.transpose(rows[r])
        for m in range(4 if r == 0 else 2):
            ggeo_out[4 * r + m] = turned[m * 32 : m * 32 + 32]


def local(features, geometry, send_lists, tile_ids, tile_lists, live_counts, cotangent):
    nt, nd = lax.axis_size("tile"), lax.axis_size("depth")
    cap = send_lists.shape[2]
    slots = nt * cap
    blocks = features.shape[0]
    picked = jnp.transpose(send_lists[0])

    vmem = pl.BlockSpec(memory_space=pltpu.VMEM)
    smem = pl.BlockSpec(memory_space=pltpu.SMEM)
    hbm = pl.BlockSpec(memory_space=pl.ANY)
    dma = pltpu.SemaphoreType.DMA
    big = pltpu.VMEM((4, 16, 256, 128), F32)
    image_out, grad_rx, ggeo_rx = pl.pallas_call(
        functools.partial(splat_kernel, nt, nd, cap),
        out_shape=(
            jax.ShapeDtypeStruct((4, 64, 128), BF16),
            jax.ShapeDtypeStruct((slots, 32, 128), BF16),
            jax.ShapeDtypeStruct((slots, 2, 128), F32),
        ),
        in_specs=[hbm, hbm, smem, smem, smem, smem, hbm],
        out_specs=(vmem, hbm, hbm),
        scratch_shapes=[
            pltpu.VMEM((blocks, 32, 128), BF16),
            pltpu.VMEM((6, blocks, 128), F32),
            pltpu.VMEM((slots, 32, 128), BF16),
            pltpu.VMEM((slots, 32, 128), BF16),
            pltpu.VMEM((16, 256, 128), BF16),
            pltpu.VMEM((2, blocks, 128), F32),
            pltpu.VMEM((slots, 2, 128), F32),
            pltpu.VMEM((slots, 2, 128), F32),
            pltpu.VMEM((nd, 8, 128), I32),
            pltpu.VMEM((8, 128), I32),
            pltpu.SMEM((nd, 8, 128), I32),
            pltpu.SMEM((8, 128), I32),
            pltpu.VMEM((2, 4, 32, 128), F32),
            pltpu.VMEM((6, 32, 128), F32),
            pltpu.VMEM((4, 256, 128), BF16),
            pltpu.VMEM((16, 256, 128), BF16),
            pltpu.VMEM((8, 256, 256), BF16),
            pltpu.VMEM((8, 256, 256), BF16),
            big,
            big,
            big,
            pltpu.VMEM((4, 8, 256, 256), BF16),
            pltpu.VMEM((256, 128), F32),
            pltpu.VMEM((4, 4, 128, 128), F32),
            pltpu.VMEM((4, 4, 128, 128), F32),
            pltpu.VMEM((256, 256), BF16),
            pltpu.VMEM((8, 256, 128), F32),
            pltpu.VMEM((slots, 32, 128), BF16),
            pltpu.VMEM((slots, 32, 128), BF16),
            pltpu.VMEM((6, 32, 128), F32),
            pltpu.VMEM((2, 4, 32, 128), F32),
            pltpu.VMEM((slots, 2, 128), F32),
            pltpu.VMEM((2, 2, 2, 128, 128), F32),
            pltpu.VMEM((nd, 2, 2, 64, 128), F32),
            dma((14,)),
            dma((2,)),
            dma((2,)),
            dma((2,)),
            dma((2,)),
            dma((nd,)),
            dma((nd,)),
            dma((2, 4)),
            dma((2, 4)),
            dma((2, 4)),
            dma((2, 4)),
            dma((nd,)),
            dma((nd,)),
        ],
        compiler_params=pltpu.CompilerParams(
            collective_id=0, has_side_effects=True, vmem_limit_bytes=62 * 1024 * 1024
        ),
        name="splat",
    )(
        features,
        jnp.transpose(geometry, (1, 0, 2)),
        picked,
        tile_ids,
        tile_lists,
        jnp.transpose(live_counts),
        cotangent,
    )

    feature_grads, geometry_grads = pl.pallas_call(
        owner_kernel,
        out_shape=(
            jax.ShapeDtypeStruct((blocks, 32, 128), F32),
            jax.ShapeDtypeStruct((6, 32, blocks), F32),
        ),
        in_specs=[smem, vmem, vmem],
        out_specs=(vmem, vmem),
        scratch_shapes=[pltpu.VMEM((2, blocks, 128), F32)],
        name="owner",
    )(picked, grad_rx, ggeo_rx)
    return image_out, feature_grads, jnp.transpose(geometry_grads, (2, 0, 1))


def solution(mesh):
    placed = (
        P("tile", None, None),
        P("tile", None, None),
        P("tile", None, None),
        P("tile"),
        P("tile", "depth", None),
        P("tile", "depth"),
        P("tile", None, None),
    )
    return jax.shard_map(
        local,
        mesh=mesh,
        in_specs=placed,
        out_specs=(P("tile", "depth", None), P("tile", "depth", None), P("tile", None, "depth")),
        check_vma=False,
    )
```

time: 91.9 us -> 89.9 us (0.978)
  local copies, waits for them, and re-layouts: 7.89 us -> 1.47 us
  Pallas kernels: 83 us -> 87.6 us
    pallas_call x1, Pallas kernels: 80.1 us -> 84.6 us  [local(): pl.pallas_call(functools.partial(splat_kernel, nt, nd, cap), out_shape=(j...]
    reshape x4 -> x0, local copies, waits for them, and re-layouts: 2.31 us -> none  [the longest x1 0.82 us: local(): tile_lists.reshape(64)]
    unnamed x6 -> x1, local copies, waits for them, and re-layouts: 3.16 us -> 1.47 us
    pallas_call x1 -> x0, local copies, waits for them, and re-layouts: 0.99 us -> none  [local(): pl.pallas_call(owner_kernel, out_shape=(jax.ShapeDtypeStruct((blocks, 32,...]
where the time goes in v2:
time: 89.9 us; the launch traced here: 89.7 us
  Pallas kernels  87.6 us (97%)
  local copies, waits for them, and re-layouts  1.47 us (2%)
    pallas_call x1, Pallas kernels, local(): pl.pallas_call(functools.partial(splat_kernel, nt, nd, cap), out_shape=(j...  84.6 us
    pallas_call x1, Pallas kernels, local(): pl.pallas_call(owner_kernel, out_shape=(jax.ShapeDtypeStruct((blocks, 32,...  2.94 us

profile of v2, /device:TPU:1, one launch (start us, length us, event | category | flops | bytes accessed | tf_op | source)
XLA Modules:
  0.0 89.7 jit_solution(1588547193568770448)
XLA Ops:
  0.6 84.6 %splat.1 = (bf16[4,64,128]{2,1,0:T(8,128)(2,1)}, bf16[128,32,128]{2,1,0:T(8,128)(2,1)}, f32[128,2,128]{2,1,0:T(2,128)}) custom-call(bf16[128,128,128]{2,1,0:T(8,128)(2,1)} %features.1, f32[6,128,128]{2,1,0:T(8,128)} %bitcast.6, s32[2,64]{1,0:T(2,128)} %bitcast.7, s32[4]{0:T(128)} %tile_ids.1, s32[4,2,8]{2,1,0:T(2,128)} %tile_lists.1, s32[2,4]{1,0:T(2,128)} %bitcast.9, ...), custom_call_target="tpu_custom_call" | custom-call | tf_op jit(solution)/shard_map/splat/pallas_call | solution.py:618
  85.3 2.9 %owner.1 = (f32[128,32,128]{2,1,0:T(8,128)}, f32[6,32,128]{2,1,0:T(8,128)}) custom-call(s32[2,64]{1,0:T(2,128)} %bitcast.8, bf16[128,32,128]{2,1,0:T(8,128)(2,1)} %get-tuple-element.9.grad_rx, f32[128,2,128]{2,1,0:T(2,128)} %get-tuple-element.10.ggeo_rx), custom_call_target="tpu_custom_call" | custom-call | tf_op jit(solution)/shard_map/owner/pallas_call | solution.py:690
  88.2 1.5 %copy.11 = bf16[4,64,128]{2,1,0:T(8,128)(2,1)} copy(bf16[4,64,128]{2,1,0:T(8,128)(2,1)} %get-tuple-element.16) | data formatting | bytes 131072

commit v3 on v2

--- a/solution.py
+++ b/solution.py
@@ -25,6 +25,19 @@
     high = value.astype(BF16)
     low = (value - high.astype(F32)).astype(BF16)
     return high, low
+
+
+def group_of(par, g, h):
+    return (g // 2) * 8 + par * 4 + (g % 2) * 2 + h
+
+
+def paired(step):
+    def both(i, c):
+        step(i * 2, c)
+        step(i * 2 + 1, c)
+        return c
+
+    return both
 
 
 def splat_kernel(
@@ -56,11 +69,13 @@
     geo_part,
     geo,
     cot,
+    cot_turned,
     place_mat,
     ahead_mat,
     behind_mat,
     fall,
     chain,
+    thru,
     later,
     weights,
     sums,
@@ -193,14 +208,6 @@
             device_id_type=MESH,
         )
 
-    pl.semaphore_wait(barrier, nt - 1 + nd - 1)
-    for step in range(1, nd):
-        peer = lax.rem(my + step, nd)
-        across_depth(
-            lists_rx.at[my], lists_rx.at[my], lists_send.at[peer], lists_recv.at[my], peer
-        ).start()
-    scatter_tiles(geo_tx, geo_rx, geo_sem)
-
     fetch_feat.wait()
 
     def pick_feat(t, c):
@@ -210,7 +217,6 @@
 
     lax.fori_loop(0, nt, pick_feat, 0, unroll=4)
     feat_rx[pl.ds(mine, cap)] = feat_tx[pl.ds(mine, cap)]
-    scatter_tiles(feat_tx, feat_rx, feat_sem)
 
     row_in = iota((256, 128), 0) % 128
     lane_out = iota((256, 128), 1)
@@ -233,6 +239,20 @@
         return c
 
     lax.fori_loop(0, 8, build, 0)
+
+    for copy in fetch_cot:
+        copy.wait()
+    for chunk in range(4):
+        cot_turned[chunk] = jnp.transpose(cot[chunk].astype(F32)).astype(BF16)
+
+    pl.semaphore_wait(barrier, nt - 1 + nd - 1)
+    for step in range(1, nd):
+        peer = lax.rem(my + step, nd)
+        across_depth(
+            lists_rx.at[my], lists_rx.at[my], lists_send.at[peer], lists_recv.at[my], peer
+        ).start()
+    scatter_tiles(geo_tx, geo_rx, geo_sem)
+    scatter_tiles(feat_tx, feat_rx, feat_sem)
 
     for step in range(1, nd):
         other = lax.rem(my + step, nd)
@@ -269,7 +289,7 @@
     def sort_geo(at, c):
         for k in range(8):
             rows = geo_rx[slot_at(at // 8, at % 8, k)]
-            group = at * 2 + k // 4
+            group = group_of(at // 8, at % 8, k // 4)
             for r in range(2):
                 geo_part[r, k % 4, pl.ds(group, 1), :] = rows[r : r + 1, :]
         return c
@@ -335,7 +355,7 @@
 
         def alpha_step(g, c, par=par, ph=ph, chunk=chunk):
             for h in range(2):
-                group = (par * 8 + g) * 2 + h
+                group = group_of(par, g, h)
                 mean_x, mean_y = row_of(0, group), row_of(1, group)
                 half_a = -0.5 * row_of(2, group)
                 minus_b = -row_of(3, group)
@@ -364,13 +384,11 @@
                 sums[...] += result[:, 128:]
             return c
 
-        lax.fori_loop(0, 8, alpha_step, 0)
+        lax.fori_loop(0, 4, paired(alpha_step), 0)
         start_near(light, light_send, light_recv, chunk)
         if chunk:
             start_far(light, light_send, light_recv, chunk - 1)
 
-    for copy in fetch_cot:
-        copy.wait()
     inv_copy.wait()
 
     for chunk in range(4):
@@ -383,27 +401,25 @@
             ahead = jnp.dot(offs[...], ahead_mat[g], preferred_element_type=F32)
             halves = []
             for h in range(2):
-                group = (par * 8 + g) * 2 + h
+                group = group_of(par, g, h)
                 opacity = jnp.broadcast_to(geo[5, pl.ds(group, 1), :], (256, 128))
                 through = jnp.exp(chain[chunk, g * 2 + h] + ahead[:, h * 128 : (h + 1) * 128])
-                chain[chunk, g * 2 + h] = through
+                thru[chunk, g * 2 + h] = through
                 halves.append((through * (opacity * fall[chunk, g * 2 + h])).astype(BF16))
             weight = jnp.concatenate(halves, axis=1)
             weights[chunk, g] = weight
-            grad = lax.dot_general(
-                weight, cot[chunk], (((0,), (0,)), ((), ())), preferred_element_type=F32
-            )
+            grad = jnp.dot(cot_turned[chunk], weight, preferred_element_type=F32)
             if ph == 0:
                 grad_sum[g] = grad
             else:
                 grad = grad + grad_sum[g]
                 at = (g // 2) * 4 + par * 2 + g % 2
-                grad_list[pl.ds(pl.multiple_of(at * 8, 8), 8)] = grad.astype(BF16).reshape(
-                    8, 32, 128
-                )
+                grad_list[pl.ds(pl.multiple_of(at * 8, 8), 8)] = jnp.transpose(grad).astype(
+                    BF16
+                ).reshape(8, 32, 128)
             return c
 
-        lax.fori_loop(0, 8, weight_step, 0)
+        lax.fori_loop(0, 4, paired(weight_step), 0)
 
     def back_feat(k, c):
         grad_tx[k] = grad_list[within(inv_sm[0, k])]
@@ -437,9 +453,9 @@
                 cot[chunk], feat, (((1,), (1,)), ((), ())), preferred_element_type=F32
             )
             for h in range(2):
-                group = (par * 8 + g) * 2 + h
+                group = group_of(par, g, h)
                 opacity = jnp.broadcast_to(geo[5, pl.ds(group, 1), :], (256, 128))
-                direct = dots[:, h * 128 : (h + 1) * 128] * chain[chunk, g * 2 + h]
+                direct = dots[:, h * 128 : (h + 1) * 128] * thru[chunk, g * 2 + h]
                 chain[chunk, g * 2 + h] = direct
                 top, rest = split_two(direct * (opacity * fall[chunk, g * 2 + h]))
                 both = jnp.concatenate([top, rest], axis=1)
@@ -449,7 +465,7 @@
                 sums[...] += result[:, 128:]
             return c
 
-        lax.fori_loop(0, 8, carry_step, 0)
+        lax.fori_loop(0, 4, paired(carry_step), 0)
         start_near(carry, carry_send, carry_recv, chunk)
         if chunk:
             start_far(carry, carry_send, carry_recv, chunk - 1)
@@ -474,7 +490,7 @@
         def shape_step(g, c, par=par, ph=ph, chunk=chunk):
             behind = jnp.dot(offs[...], behind_mat[g], preferred_element_type=F32)
             for h in range(2):
-                group = (par * 8 + g) * 2 + h
+                group = group_of(par, g, h)
                 mean_x, mean_y = row_of(0, group), row_of(1, group)
                 opacity = row_of(5, group)
                 parts = [jnp.zeros((16, 128), F32) for _ in range(6)]
@@ -511,7 +527,7 @@
                     moment[i, pl.ds(group, 1), :] = folded
             return c
 
-        lax.fori_loop(0, 8, shape_step, 0)
+        lax.fori_loop(0, 4, paired(shape_step), 0)
 
     one, sx, sy, sxx, sxy, syy = [moment[i] for i in range(6)]
     conic_a, conic_b, conic_c, opac = [geo[p] for p in (2, 3, 4, 5)]
@@ -531,15 +547,11 @@
                 part = ggeo[4 * r + m]
                 moved = pltpu.roll(part, shift, 1) if shift else part
                 total = jnp.where(lane_part == m, moved, total)
-            ggeo_list[r, i] = total
+            for group in range(32):
+                ggeo_list[group * 4 + i, r : r + 1, :] = total[group : group + 1]
 
     def back_geo(k, c):
-        at = within(inv_sm[0, k])
-        g = (at // 32) * 2 + (at // 8) % 2
-        group = (((at // 16) % 2) * 8 + g) * 2 + (at % 8) // 4
-        first = ggeo_list[0, at % 4, pl.ds(group, 1), :]
-        second = ggeo_list[1, at % 4, pl.ds(group, 1), :]
-        ggeo_tx[k] = jnp.concatenate([first, second], axis=0)
+        ggeo_tx[k] = ggeo_list[within(inv_sm[0, k])]
         return c
 
     lax.fori_loop(0, slots, back_geo, 0, unroll=8)
@@ -584,8 +596,9 @@
     all_tiles(ggeo_tx, ggeo_rx, ggeo_sem).wait()
 
 
-def owner_kernel(picked, grad_rx, ggeo_rx, grad_out, ggeo_out, rows):
+def owner_kernel(picked, grad_rx, ggeo_rx, image, grad_out, ggeo_out, image_out, rows):
     cap, nt = picked.shape
+    image_out[...] = image[...]
 
     def put(t, c):
         for j in range(cap):
@@ -615,7 +628,7 @@
     hbm = pl.BlockSpec(memory_space=pl.ANY)
     dma = pltpu.SemaphoreType.DMA
     big = pltpu.VMEM((4, 16, 256, 128), F32)
-    image_out, grad_rx, ggeo_rx = pl.pallas_call(
+    image, grad_rx, ggeo_rx = pl.pallas_call(
         functools.partial(splat_kernel, nt, nd, cap),
         out_shape=(
             jax.ShapeDtypeStruct((4, 64, 128), BF16),
@@ -640,9 +653,11 @@
             pltpu.VMEM((2, 4, 32, 128), F32),
             pltpu.VMEM((6, 32, 128), F32),
             pltpu.VMEM((4, 256, 128), BF16),
+            pltpu.VMEM((4, 128, 256), BF16),
             pltpu.VMEM((16, 256, 128), BF16),
             pltpu.VMEM((8, 256, 256), BF16),
             pltpu.VMEM((8, 256, 256), BF16),
+            big,
             big,
             big,
             big,
@@ -651,11 +666,11 @@
             pltpu.VMEM((4, 4, 128, 128), F32),
             pltpu.VMEM((4, 4, 128, 128), F32),
             pltpu.VMEM((256, 256), BF16),
-            pltpu.VMEM((8, 256, 128), F32),
+            pltpu.VMEM((8, 128, 256), F32),
             pltpu.VMEM((slots, 32, 128), BF16),
             pltpu.VMEM((slots, 32, 128), BF16),
             pltpu.VMEM((6, 32, 128), F32),
-            pltpu.VMEM((2, 4, 32, 128), F32),
+            pltpu.VMEM((slots, 2, 128), F32),
             pltpu.VMEM((slots, 2, 128), F32),
             pltpu.VMEM((2, 2, 2, 128, 128), F32),
             pltpu.VMEM((nd, 2, 2, 64, 128), F32),
@@ -687,17 +702,18 @@
         cotangent,
     )
 
-    feature_grads, geometry_grads = pl.pallas_call(
+    feature_grads, geometry_grads, image_out = pl.pallas_call(
         owner_kernel,
         out_shape=(
             jax.ShapeDtypeStruct((blocks, 32, 128), F32),
             jax.ShapeDtypeStruct((6, 32, blocks), F32),
+            jax.ShapeDtypeStruct((4, 64, 128), BF16),
         ),
-        in_specs=[smem, vmem, vmem],
-        out_specs=(vmem, vmem),
+        in_specs=[smem, vmem, vmem, vmem],
+        out_specs=(vmem, vmem, vmem),
         scratch_shapes=[pltpu.VMEM((2, blocks, 128), F32)],
         name="owner",
-    )(picked, grad_rx, ggeo_rx)
+    )(picked, grad_rx, ggeo_rx, image)
     return image_out, feature_grads, jnp.transpose(geometry_grads, (2, 0, 1))
 
 

time: 89.9 us -> 79.5 us (0.88)
  Pallas kernels: 87.6 us -> 78.7 us
  local copies, waits for them, and re-layouts: 1.47 us -> 0 us
    pallas_call x1, Pallas kernels: 84.6 us -> 75.7 us  [local(): pl.pallas_call(functools.partial(splat_kernel, nt, nd, cap), out_shape=(j...]
    unnamed x1 -> x0, local copies, waits for them, and re-layouts: 1.47 us -> none
where the time goes in v3:
time: 79.5 us; the launch traced here: 79.3 us
  Pallas kernels  78.7 us (99%)
    pallas_call x1, Pallas kernels, local(): pl.pallas_call(functools.partial(splat_kernel, nt, nd, cap), out_shape=(j...  75.7 us
    pallas_call x1, Pallas kernels, local(): pl.pallas_call(owner_kernel, out_shape=(jax.ShapeDtypeStruct((blocks, 32,...  3.04 us

profile of v3, /device:TPU:1, one launch (start us, length us, event | category | flops | bytes accessed | tf_op | source)
XLA Modules:
  0.0 79.3 jit_solution(3465699252501317605)
XLA Ops:
  0.6 75.7 %splat.1 = (bf16[4,64,128]{2,1,0:T(8,128)(2,1)}, bf16[128,32,128]{2,1,0:T(8,128)(2,1)}, f32[128,2,128]{2,1,0:T(2,128)}) custom-call(bf16[128,128,128]{2,1,0:T(8,128)(2,1)} %features.1, f32[6,128,128]{2,1,0:T(8,128)} %bitcast.6, s32[2,64]{1,0:T(2,128)} %bitcast.7, s32[4]{0:T(128)} %tile_ids.1, s32[4,2,8]{2,1,0:T(2,128)} %tile_lists.1, s32[2,4]{1,0:T(2,128)} %bitcast.9, ...), custom_call_target="tpu_custom_call" | custom-call | tf_op jit(solution)/shard_map/splat/pallas_call | solution.py:631
  76.3 3.0 %owner.1 = (f32[128,32,128]{2,1,0:T(8,128)}, f32[6,32,128]{2,1,0:T(8,128)}, bf16[4,64,128]{2,1,0:T(8,128)(2,1)}) custom-call(s32[2,64]{1,0:T(2,128)} %bitcast.8, bf16[128,32,128]{2,1,0:T(8,128)(2,1)} %get-tuple-element.9.grad_rx, f32[128,2,128]{2,1,0:T(2,128)} %get-tuple-element.10.ggeo_rx, bf16[4,64,128]{2,1,0:T(8,128)(2,1)} %get-tuple-element.11.image), custom_call_target="tpu_custom_call" | custom-call | tf_op jit(solution)/shard_map/owner/pallas_call | solution.py:705

commit v4 on v3

--- a/solution.py
+++ b/solution.py
@@ -31,13 +31,26 @@
     return (g // 2) * 8 + par * 4 + (g % 2) * 2 + h
 
 
-def paired(step):
-    def both(i, c):
-        step(i * 2, c)
-        step(i * 2 + 1, c)
-        return c
-
-    return both
+def groups(step, many):
+    def several(i, c):
+        for k in range(many):
+            step(i * many + k, c)
+        return c
+
+    lax.fori_loop(0, 8 // many, several, 0)
+
+
+def chained(first, second, many):
+    def several(i, c):
+        coming = first(i * many)
+        for k in range(many):
+            ready = coming
+            if k + 1 < many:
+                coming = first(i * many + k + 1)
+            second(i * many + k, ready)
+        return c
+
+    lax.fori_loop(0, 8 // many, several, 0)
 
 
 def splat_kernel(
@@ -384,21 +397,23 @@
                 sums[...] += result[:, 128:]
             return c
 
-        lax.fori_loop(0, 4, paired(alpha_step), 0)
+        groups(alpha_step, 4)
         start_near(light, light_send, light_recv, chunk)
-        if chunk:
-            start_far(light, light_send, light_recv, chunk - 1)
+        if chunk >= 2:
+            start_far(light, light_send, light_recv, chunk - 2)
 
     inv_copy.wait()
 
     for chunk in range(4):
         par, ph = chunk // 2, chunk % 2
-        if chunk == 1:
-            start_far(light, light_send, light_recv, 3)
+        if 1 <= chunk <= 2:
+            start_far(light, light_send, light_recv, chunk + 1)
         offsets_from(light, light_send, light_recv, chunk, odd, upper)
 
-        def weight_step(g, c, par=par, ph=ph, chunk=chunk):
-            ahead = jnp.dot(offs[...], ahead_mat[g], preferred_element_type=F32)
+        def weight_ahead(g):
+            return jnp.dot(offs[...], ahead_mat[g], preferred_element_type=F32)
+
+        def weight_step(g, ahead, par=par, ph=ph, chunk=chunk):
             halves = []
             for h in range(2):
                 group = group_of(par, g, h)
@@ -417,9 +432,8 @@
                 grad_list[pl.ds(pl.multiple_of(at * 8, 8), 8)] = jnp.transpose(grad).astype(
                     BF16
                 ).reshape(8, 32, 128)
-            return c
-
-        lax.fori_loop(0, 4, paired(weight_step), 0)
+
+        chained(weight_ahead, weight_step, 4)
 
     def back_feat(k, c):
         grad_tx[k] = grad_list[within(inv_sm[0, k])]
@@ -445,13 +459,15 @@
         par, ph = chunk // 2, chunk % 2
         sums[...] = jnp.zeros((256, 128), F32)
 
-        def carry_step(g, c, par=par, ph=ph, chunk=chunk):
+        def carry_ahead(g, par=par, ph=ph, chunk=chunk):
             feat = feat_list[par * 8 + g]
             shown = jnp.dot(weights[chunk, g], feat, preferred_element_type=F32)
             image_part[par, ph] += shown.reshape(2, 128, 128)
-            dots = lax.dot_general(
+            return lax.dot_general(
                 cot[chunk], feat, (((1,), (1,)), ((), ())), preferred_element_type=F32
             )
+
+        def carry_step(g, dots, par=par, chunk=chunk):
             for h in range(2):
                 group = group_of(par, g, h)
                 opacity = jnp.broadcast_to(geo[5, pl.ds(group, 1), :], (256, 128))
@@ -463,9 +479,8 @@
                 result = jnp.dot(both, right, preferred_element_type=F32)
                 later[chunk, g * 2 + h] = result[:, :128]
                 sums[...] += result[:, 128:]
-            return c
-
-        lax.fori_loop(0, 4, paired(carry_step), 0)
+
+        chained(carry_ahead, carry_step, 4)
         start_near(carry, carry_send, carry_recv, chunk)
         if chunk:
             start_far(carry, carry_send, carry_recv, chunk - 1)
@@ -527,7 +542,7 @@
                     moment[i, pl.ds(group, 1), :] = folded
             return c
 
-        lax.fori_loop(0, 4, paired(shape_step), 0)
+        groups(shape_step, 4)
 
     one, sx, sy, sxx, sxy, syy = [moment[i] for i in range(6)]
     conic_a, conic_b, conic_c, opac = [geo[p] for p in (2, 3, 4, 5)]

time: 79.5 us -> 73.8 us (0.928)
  Pallas kernels: 78.7 us -> 72.6 us
    pallas_call x1, Pallas kernels: 75.7 us -> 69.5 us  [local(): pl.pallas_call(functools.partial(splat_kernel, nt, nd, cap), out_shape=(j...]
where the time goes in v4:
time: 73.8 us; the launch traced here: 73.2 us
  Pallas kernels  72.6 us (98%)
    pallas_call x1, Pallas kernels, local(): pl.pallas_call(functools.partial(splat_kernel, nt, nd, cap), out_shape=(j...  69.5 us
    pallas_call x1, Pallas kernels, local(): pl.pallas_call(owner_kernel, out_shape=(jax.ShapeDtypeStruct((blocks, 32,...  3.04 us

profile of v4, /device:TPU:1, one launch (start us, length us, event | category | flops | bytes accessed | tf_op | source)
XLA Modules:
  0.0 73.2 jit_solution(15679950792785070160)
XLA Ops:
  0.6 69.5 %splat.1 = (bf16[4,64,128]{2,1,0:T(8,128)(2,1)}, bf16[128,32,128]{2,1,0:T(8,128)(2,1)}, f32[128,2,128]{2,1,0:T(2,128)}) custom-call(bf16[128,128,128]{2,1,0:T(8,128)(2,1)} %features.1, f32[6,128,128]{2,1,0:T(8,128)} %bitcast.6, s32[2,64]{1,0:T(2,128)} %bitcast.7, s32[4]{0:T(128)} %tile_ids.1, s32[4,2,8]{2,1,0:T(2,128)} %tile_lists.1, s32[2,4]{1,0:T(2,128)} %bitcast.9, ...), custom_call_target="tpu_custom_call" | custom-call | tf_op jit(solution)/shard_map/splat/pallas_call | solution.py:646
  70.2 3.0 %owner.1 = (f32[128,32,128]{2,1,0:T(8,128)}, f32[6,32,128]{2,1,0:T(8,128)}, bf16[4,64,128]{2,1,0:T(8,128)(2,1)}) custom-call(s32[2,64]{1,0:T(2,128)} %bitcast.8, bf16[128,32,128]{2,1,0:T(8,128)(2,1)} %get-tuple-element.9.grad_rx, f32[128,2,128]{2,1,0:T(2,128)} %get-tuple-element.10.ggeo_rx, bf16[4,64,128]{2,1,0:T(8,128)(2,1)} %get-tuple-element.11.image), custom_call_target="tpu_custom_call" | custom-call | tf_op jit(solution)/shard_map/owner/pallas_call | solution.py:720

commit v5 on v4

--- a/solution.py
+++ b/solution.py
@@ -362,78 +362,90 @@
     odd = jnp.where(my % 2 == 1, 1.0, 0.0)
     upper = jnp.where(my >= 2, 1.0, 0.0)
 
-    for chunk in range(4):
-        par, ph = chunk // 2, chunk % 2
-        sums[...] = jnp.zeros((256, 128), F32)
-
-        def alpha_step(g, c, par=par, ph=ph, chunk=chunk):
-            for h in range(2):
-                group = group_of(par, g, h)
-                mean_x, mean_y = row_of(0, group), row_of(1, group)
-                half_a = -0.5 * row_of(2, group)
-                minus_b = -row_of(3, group)
-                half_c = -0.5 * row_of(4, group)
-                opacity = row_of(5, group)
-                highs, lows = [], []
-                for high in range(2):
-                    tile = high * 2 + par
-                    dx = column - (mean_x - origin(tile))
-                    alive = entry_lane + h * 4 < live_at(tile, g)
-                    ax = jnp.where(alive, half_a * dx * dx, -1e30)
-                    for py in range(8):
-                        dy = (py + ph * 8 + 0.5) - mean_y
-                        power = dx * (minus_b * dy) + (ax + half_c * dy * dy)
-                        falloff = jnp.exp(power)
-                        fall[chunk, g * 2 + h, pl.ds(high * 128 + py * 16, 16), :] = falloff
-                        top, rest = split_two(jnp.log(1.0 - opacity * falloff))
-                        highs.append(top)
-                        lows.append(rest)
-                both = jnp.concatenate(
-                    [jnp.concatenate(highs, axis=0), jnp.concatenate(lows, axis=0)], axis=1
-                )
-                right = jnp.concatenate([before_mat, place_mat[g * 2 + h]], axis=1)
-                result = jnp.dot(both, right, preferred_element_type=F32)
-                chain[chunk, g * 2 + h] = result[:, :128]
-                sums[...] += result[:, 128:]
-            return c
-
-        groups(alpha_step, 4)
-        start_near(light, light_send, light_recv, chunk)
-        if chunk >= 2:
-            start_far(light, light_send, light_recv, chunk - 2)
+    def phase_1(par, c):
+        for ph in range(2):
+            chunk = par * 2 + ph
+            sums[...] = jnp.zeros((256, 128), F32)
+
+            def alpha_step(g, c, par=par, ph=ph, chunk=chunk):
+                for h in range(2):
+                    group = group_of(par, g, h)
+                    mean_x, mean_y = row_of(0, group), row_of(1, group)
+                    half_a = -0.5 * row_of(2, group)
+                    minus_b = -row_of(3, group)
+                    half_c = -0.5 * row_of(4, group)
+                    opacity = row_of(5, group)
+                    highs, lows = [], []
+                    for high in range(2):
+                        tile = high * 2 + par
+                        dx = column - (mean_x - origin(tile))
+                        alive = entry_lane + h * 4 < live_at(tile, g)
+                        ax = jnp.where(alive, half_a * dx * dx, -1e30)
+                        for py in range(8):
+                            dy = (py + ph * 8 + 0.5) - mean_y
+                            power = dx * (minus_b * dy) + (ax + half_c * dy * dy)
+                            falloff = jnp.exp(power)
+                            fall[chunk, g * 2 + h, pl.ds(high * 128 + py * 16, 16), :] = falloff
+                            top, rest = split_two(jnp.log(1.0 - opacity * falloff))
+                            highs.append(top)
+                            lows.append(rest)
+                    both = jnp.concatenate(
+                        [jnp.concatenate(highs, axis=0), jnp.concatenate(lows, axis=0)], axis=1
+                    )
+                    right = jnp.concatenate([before_mat, place_mat[g * 2 + h]], axis=1)
+                    result = jnp.dot(both, right, preferred_element_type=F32)
+                    chain[chunk, g * 2 + h] = result[:, :128]
+                    sums[...] += result[:, 128:]
+                return c
+
+            groups(alpha_step, 4)
+            start_near(light, light_send, light_recv, chunk)
+
+            @pl.when(par == 1)
+            def _(ph=ph):
+                start_far(light, light_send, light_recv, ph)
+        return c
+
+    lax.fori_loop(0, 2, phase_1, 0)
 
     inv_copy.wait()
 
-    for chunk in range(4):
-        par, ph = chunk // 2, chunk % 2
-        if 1 <= chunk <= 2:
-            start_far(light, light_send, light_recv, chunk + 1)
-        offsets_from(light, light_send, light_recv, chunk, odd, upper)
-
-        def weight_ahead(g):
-            return jnp.dot(offs[...], ahead_mat[g], preferred_element_type=F32)
-
-        def weight_step(g, ahead, par=par, ph=ph, chunk=chunk):
-            halves = []
-            for h in range(2):
-                group = group_of(par, g, h)
-                opacity = jnp.broadcast_to(geo[5, pl.ds(group, 1), :], (256, 128))
-                through = jnp.exp(chain[chunk, g * 2 + h] + ahead[:, h * 128 : (h + 1) * 128])
-                thru[chunk, g * 2 + h] = through
-                halves.append((through * (opacity * fall[chunk, g * 2 + h])).astype(BF16))
-            weight = jnp.concatenate(halves, axis=1)
-            weights[chunk, g] = weight
-            grad = jnp.dot(cot_turned[chunk], weight, preferred_element_type=F32)
-            if ph == 0:
-                grad_sum[g] = grad
-            else:
-                grad = grad + grad_sum[g]
-                at = (g // 2) * 4 + par * 2 + g % 2
-                grad_list[pl.ds(pl.multiple_of(at * 8, 8), 8)] = jnp.transpose(grad).astype(
-                    BF16
-                ).reshape(8, 32, 128)
-
-        chained(weight_ahead, weight_step, 4)
+    def phase_2(par, c):
+        for ph in range(2):
+            chunk = par * 2 + ph
+            @pl.when(par == 1 - ph)
+            def _(ph=ph):
+                start_far(light, light_send, light_recv, 3 - ph)
+
+            offsets_from(light, light_send, light_recv, chunk, odd, upper)
+
+            def weight_ahead(g):
+                return jnp.dot(offs[...], ahead_mat[g], preferred_element_type=F32)
+
+            def weight_step(g, ahead, par=par, ph=ph, chunk=chunk):
+                halves = []
+                for h in range(2):
+                    group = group_of(par, g, h)
+                    opacity = jnp.broadcast_to(geo[5, pl.ds(group, 1), :], (256, 128))
+                    through = jnp.exp(chain[chunk, g * 2 + h] + ahead[:, h * 128 : (h + 1) * 128])
+                    thru[chunk, g * 2 + h] = through
+                    halves.append((through * (opacity * fall[chunk, g * 2 + h])).astype(BF16))
+                weight = jnp.concatenate(halves, axis=1)
+                weights[chunk, g] = weight
+                grad = jnp.dot(cot_turned[chunk], weight, preferred_element_type=F32)
+                if ph == 0:
+                    grad_sum[g] = grad
+                else:
+                    grad = grad + grad_sum[g]
+                    at = (g // 2) * 4 + par * 2 + g % 2
+                    grad_list[pl.ds(pl.multiple_of(at * 8, 8), 8)] = jnp.transpose(grad).astype(
+                        BF16
+                    ).reshape(8, 32, 128)
+
+            chained(weight_ahead, weight_step, 4)
+        return c
+
+    lax.fori_loop(0, 2, phase_2, 0)
 
     def back_feat(k, c):
         grad_tx[k] = grad_list[within(inv_sm[0, k])]
@@ -455,94 +467,111 @@
     lax.fori_loop(0, 16, sort_feat, 0)
     image_part[...] = jnp.zeros(image_part.shape, F32)
 
-    for chunk in range(4):
-        par, ph = chunk // 2, chunk % 2
-        sums[...] = jnp.zeros((256, 128), F32)
-
-        def carry_ahead(g, par=par, ph=ph, chunk=chunk):
-            feat = feat_list[par * 8 + g]
-            shown = jnp.dot(weights[chunk, g], feat, preferred_element_type=F32)
-            image_part[par, ph] += shown.reshape(2, 128, 128)
-            return lax.dot_general(
-                cot[chunk], feat, (((1,), (1,)), ((), ())), preferred_element_type=F32
-            )
-
-        def carry_step(g, dots, par=par, chunk=chunk):
-            for h in range(2):
-                group = group_of(par, g, h)
-                opacity = jnp.broadcast_to(geo[5, pl.ds(group, 1), :], (256, 128))
-                direct = dots[:, h * 128 : (h + 1) * 128] * thru[chunk, g * 2 + h]
-                chain[chunk, g * 2 + h] = direct
-                top, rest = split_two(direct * (opacity * fall[chunk, g * 2 + h]))
-                both = jnp.concatenate([top, rest], axis=1)
-                right = jnp.concatenate([after_mat, place_mat[g * 2 + h]], axis=1)
-                result = jnp.dot(both, right, preferred_element_type=F32)
-                later[chunk, g * 2 + h] = result[:, :128]
-                sums[...] += result[:, 128:]
-
-        chained(carry_ahead, carry_step, 4)
-        start_near(carry, carry_send, carry_recv, chunk)
-        if chunk:
-            start_far(carry, carry_send, carry_recv, chunk - 1)
-
-    for chunk in range(4):
-        par, ph = chunk // 2, chunk % 2
-        if chunk == 1:
-            start_far(carry, carry_send, carry_recv, 3)
-            for step in range(1, nd):
-                peer = lax.rem(my + step, nd)
-                across_depth(
-                    image_part.at[
-                        :, peer // 2, :, pl.ds(pl.multiple_of((peer % 2) * 64, 64), 64), :
-                    ],
-                    image_rx.at[my],
-                    image_send.at[peer],
-                    image_recv.at[my],
-                    peer,
-                ).start()
-        offsets_from(carry, carry_send, carry_recv, chunk, 1.0 - odd, 1.0 - upper)
-
-        def shape_step(g, c, par=par, ph=ph, chunk=chunk):
-            behind = jnp.dot(offs[...], behind_mat[g], preferred_element_type=F32)
-            for h in range(2):
-                group = group_of(par, g, h)
-                mean_x, mean_y = row_of(0, group), row_of(1, group)
-                opacity = row_of(5, group)
-                parts = [jnp.zeros((16, 128), F32) for _ in range(6)]
-                for high in range(2):
-                    tile = high * 2 + par
-                    dx = column - (mean_x - origin(tile))
-                    flat = jnp.zeros((16, 128), F32)
-                    tilt = jnp.zeros((16, 128), F32)
-                    bend = jnp.zeros((16, 128), F32)
-                    for py in range(8):
-                        at = high * 128 + py * 16
-                        rows = pl.ds(at, 16)
-                        dy = (py + ph * 8 + 0.5) - mean_y
-                        falloff = fall[chunk, g * 2 + h, rows, :]
-                        after = (
-                            later[chunk, g * 2 + h, rows, :]
-                            + behind[at : at + 16, h * 128 : (h + 1) * 128]
-                        )
-                        alpha_grad = chain[chunk, g * 2 + h, rows, :] - after / (
-                            1.0 - opacity * falloff
-                        )
-                        term = alpha_grad * falloff
-                        term_y = term * dy
-                        flat = flat + term
-                        tilt = tilt + term_y
-                        bend = bend + term_y * dy
-                    flat_x = flat * dx
-                    adds = [flat, flat_x, tilt, flat_x * dx, tilt * dx, bend]
-                    parts = [a + b for a, b in zip(parts, adds)]
-                for i, part in enumerate(parts):
-                    folded = jnp.sum(part, axis=0, keepdims=True)
-                    if ph:
-                        folded = folded + moment[i, pl.ds(group, 1), :]
-                    moment[i, pl.ds(group, 1), :] = folded
-            return c
-
-        groups(shape_step, 4)
+    def phase_3(par, c):
+        for ph in range(2):
+            chunk = par * 2 + ph
+            sums[...] = jnp.zeros((256, 128), F32)
+
+            def carry_ahead(g, par=par, ph=ph, chunk=chunk):
+                feat = feat_list[par * 8 + g]
+                shown = jnp.dot(weights[chunk, g], feat, preferred_element_type=F32)
+                image_part[par, ph] += shown.reshape(2, 128, 128)
+                return lax.dot_general(
+                    cot[chunk], feat, (((1,), (1,)), ((), ())), preferred_element_type=F32
+                )
+
+            def carry_step(g, dots, par=par, chunk=chunk):
+                for h in range(2):
+                    group = group_of(par, g, h)
+                    opacity = jnp.broadcast_to(geo[5, pl.ds(group, 1), :], (256, 128))
+                    direct = dots[:, h * 128 : (h + 1) * 128] * thru[chunk, g * 2 + h]
+                    chain[chunk, g * 2 + h] = direct
+                    top, rest = split_two(direct * (opacity * fall[chunk, g * 2 + h]))
+                    both = jnp.concatenate([top, rest], axis=1)
+                    right = jnp.concatenate([after_mat, place_mat[g * 2 + h]], axis=1)
+                    result = jnp.dot(both, right, preferred_element_type=F32)
+                    later[chunk, g * 2 + h] = result[:, :128]
+                    sums[...] += result[:, 128:]
+
+            chained(carry_ahead, carry_step, 4)
+            start_near(carry, carry_send, carry_recv, chunk)
+            if ph:
+                start_far(carry, carry_send, carry_recv, par * 2)
+            else:
+
+                @pl.when(par == 1)
+                def _():
+                    start_far(carry, carry_send, carry_recv, 1)
+        return c
+
+    lax.fori_loop(0, 2, phase_3, 0)
+
+    def phase_4(par, c):
+        for ph in range(2):
+            chunk = par * 2 + ph
+            if ph:
+
+                @pl.when(par == 0)
+                def _():
+                    start_far(carry, carry_send, carry_recv, 3)
+                    for step in range(1, nd):
+                        peer = lax.rem(my + step, nd)
+                        across_depth(
+                            image_part.at[
+                                :, peer // 2, :, pl.ds(pl.multiple_of((peer % 2) * 64, 64), 64), :
+                            ],
+                            image_rx.at[my],
+                            image_send.at[peer],
+                            image_recv.at[my],
+                            peer,
+                        ).start()
+
+            offsets_from(carry, carry_send, carry_recv, chunk, 1.0 - odd, 1.0 - upper)
+
+            def shape_step(g, c, par=par, ph=ph, chunk=chunk):
+                behind = jnp.dot(offs[...], behind_mat[g], preferred_element_type=F32)
+                for h in range(2):
+                    group = group_of(par, g, h)
+                    mean_x, mean_y = row_of(0, group), row_of(1, group)
+                    opacity = row_of(5, group)
+                    parts = [jnp.zeros((16, 128), F32) for _ in range(6)]
+                    for high in range(2):
+                        tile = high * 2 + par
+                        dx = column - (mean_x - origin(tile))
+                        flat = jnp.zeros((16, 128), F32)
+                        tilt = jnp.zeros((16, 128), F32)
+                        bend = jnp.zeros((16, 128), F32)
+                        for py in range(8):
+                            at = high * 128 + py * 16
+                            rows = pl.ds(at, 16)
+                            dy = (py + ph * 8 + 0.5) - mean_y
+                            falloff = fall[chunk, g * 2 + h, rows, :]
+                            after = (
+                                later[chunk, g * 2 + h, rows, :]
+                                + behind[at : at + 16, h * 128 : (h + 1) * 128]
+                            )
+                            alpha_grad = chain[chunk, g * 2 + h, rows, :] - after / (
+                                1.0 - opacity * falloff
+                            )
+                            term = alpha_grad * falloff
+                            term_y = term * dy
+                            flat = flat + term
+                            tilt = tilt + term_y
+                            bend = bend + term_y * dy
+                        flat_x = flat * dx
+                        adds = [flat, flat_x, tilt, flat_x * dx, tilt * dx, bend]
+                        parts = [a + b for a, b in zip(parts, adds)]
+                    for i, part in enumerate(parts):
+                        folded = jnp.sum(part, axis=0, keepdims=True)
+                        if ph:
+                            folded = folded + moment[i, pl.ds(group, 1), :]
+                        moment[i, pl.ds(group, 1), :] = folded
+                return c
+
+            groups(shape_step, 4)
+        return c
+
+    lax.fori_loop(0, 2, phase_4, 0)
 
     one, sx, sy, sxx, sxy, syy = [moment[i] for i in range(6)]
     conic_a, conic_b, conic_c, opac = [geo[p] for p in (2, 3, 4, 5)]

time: 73.8 us -> 73.8 us (level)
  no operation moved by 1% of the time
where the time goes in v5:
time: 73.8 us; the launch traced here: 73.3 us
  Pallas kernels  72.6 us (98%)
    pallas_call x1, Pallas kernels, local(): pl.pallas_call(functools.partial(splat_kernel, nt, nd, cap), out_shape=(j...  69.6 us
    pallas_call x1, Pallas kernels, local(): pl.pallas_call(owner_kernel, out_shape=(jax.ShapeDtypeStruct((blocks, 32,...  3.04 us

profile of v5, /device:TPU:1, one launch (start us, length us, event | category | flops | bytes accessed | tf_op | source)
XLA Modules:
  0.0 73.3 jit_solution(8298394133276748278)
XLA Ops:
  0.6 69.6 %splat.1 = (bf16[4,64,128]{2,1,0:T(8,128)(2,1)}, bf16[128,32,128]{2,1,0:T(8,128)(2,1)}, f32[128,2,128]{2,1,0:T(2,128)}) custom-call(bf16[128,128,128]{2,1,0:T(8,128)(2,1)} %features.1, f32[6,128,128]{2,1,0:T(8,128)} %bitcast.6, s32[2,64]{1,0:T(2,128)} %bitcast.7, s32[4]{0:T(128)} %tile_ids.1, s32[4,2,8]{2,1,0:T(2,128)} %tile_lists.1, s32[2,4]{1,0:T(2,128)} %bitcast.9, ...), custom_call_target="tpu_custom_call" | custom-call | tf_op jit(solution)/shard_map/splat/pallas_call | solution.py:675
  70.2 3.0 %owner.1 = (f32[128,32,128]{2,1,0:T(8,128)}, f32[6,32,128]{2,1,0:T(8,128)}, bf16[4,64,128]{2,1,0:T(8,128)(2,1)}) custom-call(s32[2,64]{1,0:T(2,128)} %bitcast.8, bf16[128,32,128]{2,1,0:T(8,128)(2,1)} %get-tuple-element.9.grad_rx, f32[128,2,128]{2,1,0:T(2,128)} %get-tuple-element.10.ggeo_rx, bf16[4,64,128]{2,1,0:T(8,128)(2,1)} %get-tuple-element.11.image), custom_call_target="tpu_custom_call" | custom-call | tf_op jit(solution)/shard_map/owner/pallas_call | solution.py:749

commit v6 on v5

--- a/solution.py
+++ b/solution.py
@@ -640,24 +640,42 @@
     all_tiles(ggeo_tx, ggeo_rx, ggeo_sem).wait()
 
 
-def owner_kernel(picked, grad_rx, ggeo_rx, image, grad_out, ggeo_out, image_out, rows):
+def owner_kernel(picked, grad_rx, ggeo_rx, image, grad_out, ggeo_out, image_out, held, wide, rows, sems):
     cap, nt = picked.shape
+    parts = 4
+    many = nt // parts
+    fetches = []
+    for part in range(parts):
+        span = pl.ds(part * many * cap, many * cap)
+        fetch = pltpu.make_async_copy(grad_rx.at[span], held.at[span], sems.at[part])
+        fetch.start()
+        fetches.append(fetch)
     image_out[...] = image[...]
+
+    def widen(t, c):
+        for j in range(cap):
+            k = t * cap + j
+            wide[k] = held[k].astype(F32)
+        return c
 
     def put(t, c):
         for j in range(cap):
             k = t * cap + j
             at = picked[j, t]
-            grad_out[at] = grad_rx[k].astype(F32)
+            pltpu.make_async_copy(wide.at[k], grad_out.at[at], sems.at[parts]).start()
             for r in range(2):
                 rows[r, pl.ds(at, 1), :] = ggeo_rx[k, r : r + 1, :]
         return c
 
-    lax.fori_loop(0, nt, put, 0, unroll=4)
+    for part in range(parts):
+        fetches[part].wait()
+        lax.fori_loop(part * many, part * many + many, widen, 0, unroll=4)
+        lax.fori_loop(part * many, part * many + many, put, 0, unroll=4)
     for r in range(2):
         turned = jnp.transpose(rows[r])
         for m in range(4 if r == 0 else 2):
             ggeo_out[4 * r + m] = turned[m * 32 : m * 32 + 32]
+    pltpu.make_async_copy(wide, grad_out, sems.at[parts]).wait()
 
 
 def local(features, geometry, send_lists, tile_ids, tile_lists, live_counts, cotangent):
@@ -753,9 +771,14 @@
             jax.ShapeDtypeStruct((6, 32, blocks), F32),
             jax.ShapeDtypeStruct((4, 64, 128), BF16),
         ),
-        in_specs=[smem, vmem, vmem, vmem],
-        out_specs=(vmem, vmem, vmem),
-        scratch_shapes=[pltpu.VMEM((2, blocks, 128), F32)],
+        in_specs=[smem, hbm, vmem, vmem],
+        out_specs=(hbm, vmem, vmem),
+        scratch_shapes=[
+            pltpu.VMEM((slots, 32, 128), BF16),
+            pltpu.VMEM((slots, 32, 128), F32),
+            pltpu.VMEM((2, blocks, 128), F32),
+            dma((5,)),
+        ],
         name="owner",
     )(picked, grad_rx, ggeo_rx, image)
     return image_out, feature_grads, jnp.transpose(geometry_grads, (2, 0, 1))

time: 73.8 us -> 74.7 us (1.012)
  Pallas kernels: 72.6 us -> 73.5 us
    pallas_call x1, Pallas kernels: 3.04 us -> 3.89 us  [local(): pl.pallas_call(owner_kernel, out_shape=(jax.ShapeDtypeStruct((blocks, 32,...]
where the time goes in v6:
time: 74.7 us; the launch traced here: 74.1 us
  Pallas kernels  73.5 us (98%)
    pallas_call x1, Pallas kernels, local(): pl.pallas_call(functools.partial(splat_kernel, nt, nd, cap), out_shape=(j...  69.6 us
    pallas_call x1, Pallas kernels, local(): pl.pallas_call(owner_kernel, out_shape=(jax.ShapeDtypeStruct((blocks, 32,...  3.89 us

profile of v6, /device:TPU:1, one launch (start us, length us, event | category | flops | bytes accessed | tf_op | source)
XLA Modules:
  0.0 74.1 jit_solution(7664287966306398377)
XLA Ops:
  0.6 69.6 %splat.1 = (bf16[4,64,128]{2,1,0:T(8,128)(2,1)}, bf16[128,32,128]{2,1,0:T(8,128)(2,1)}, f32[128,2,128]{2,1,0:T(2,128)}) custom-call(bf16[128,128,128]{2,1,0:T(8,128)(2,1)} %features.1, f32[6,128,128]{2,1,0:T(8,128)} %bitcast.6, s32[2,64]{1,0:T(2,128)} %bitcast.7, s32[4]{0:T(128)} %tile_ids.1, s32[4,2,8]{2,1,0:T(2,128)} %tile_lists.1, s32[2,4]{1,0:T(2,128)} %bitcast.9, ...), custom_call_target="tpu_custom_call" | custom-call | tf_op jit(solution)/shard_map/splat/pallas_call | solution.py:693
  70.2 3.9 %owner.1 = (f32[128,32,128]{2,1,0:T(8,128)}, f32[6,32,128]{2,1,0:T(8,128)}, bf16[4,64,128]{2,1,0:T(8,128)(2,1)}) custom-call(s32[2,64]{1,0:T(2,128)} %bitcast.8, bf16[128,32,128]{2,1,0:T(8,128)(2,1)} %get-tuple-element.9.grad_rx, f32[128,2,128]{2,1,0:T(2,128)} %get-tuple-element.10.ggeo_rx, bf16[4,64,128]{2,1,0:T(8,128)(2,1)} %get-tuple-element.11.image), custom_call_target="tpu_custom_call" | custom-call | tf_op jit(solution)/shard_map/owner/pallas_call | solution.py:767
